TPU v7x, 32 devices: a whole 2x2x4 slice. The times are simulated.
32 devices in a mesh: dp: 2 (over core), row: 4 (over y, x), col: 4 (over z).
Axes of the slice: x: 2, y: 2, z: 4, core: 2. Of those that a mesh axis runs over, the one named last changes fastest.
Arguments:
- x_stream: bfloat16 [512, 16384], P('col', ('dp', 'row')), may hold values from -6 to 6
- y_stream: bfloat16 [512, 16384], P('col', ('dp', 'row')), may hold values from -6 to 6
- w_qkv: bfloat16 [512, 3, 512], P('col', None, 'row'), may hold values from -0.25 to 0.25
- w_out: bfloat16 [512, 512], P('row', 'col'), may hold values from -4 to 4
- gain_attn: bfloat16 [512], P('col'), may hold values from 0.25 to 1.75
- bias_attn: bfloat16 [512], P('col'), may hold values from -3 to 3
- w_up: bfloat16 [512, 2048], P('col', 'row'), may hold values from -0.25 to 0.25
- w_down: bfloat16 [2048, 512], P('row', 'col'), may hold values from -0.1875 to 0.1875
- gain_ffn: bfloat16 [512], P('col'), may hold values from 0.25 to 1.75
- bias_ffn: bfloat16 [512], P('col'), may hold values from -3 to 3
- teach_x: bfloat16 [512, 16384], P('col', ('dp', 'row')), may hold values from -6 to 6
- teach_y: bfloat16 [512, 16384], P('col', ('dp', 'row')), may hold values from -9 to 9
- lengths: int32 [8, 9], replicated, may hold values from 1 to 1024, as said below
Outputs:
- x_out: bfloat16 [512, 16384], P('col', ('dp', 'row'))
- y_out: bfloat16 [512, 16384], P('col', ('dp', 'row'))
- grad_x: float32 [512, 16384], P('col', ('dp', 'row'))
- grad_y: float32 [512, 16384], P('col', ('dp', 'row'))
- grad_w_qkv: float32 [512, 3, 512], P('col', None, 'row')
- grad_w_out: float32 [512, 512], P('row', 'col')
- grad_gain_attn: float32 [512], P('col')
- grad_bias_attn: float32 [512], P('col')
- grad_w_up: float32 [512, 2048], P('col', 'row')
- grad_w_down: float32 [2048, 512], P('row', 'col')
- grad_gain_ffn: float32 [512], P('col')
- grad_bias_ffn: float32 [512], P('col')
- loss: float32 [], replicated
Inputs may be any that keep to these rules, and one draw needn't show every extreme that they name: Prompt lengths lie in 512 to 1024 and continuation lengths in 1 to 128; group 0 has a full prompt and a full first continuation.
All inputs are finite; a program needn't handle non-finite values.
Results may differ from a plain program's by a relative error of at most 0.01115.
Values may be sent and summed in bfloat16 or wider, within the bound.
A program may use at most 256 MiB of HBM per device.

v0:
```python
import functools

import jax
import jax.numpy as jnp
from jax import lax
from jax.experimental import pallas as pl
from jax.experimental.pallas import tpu as pltpu
from jax.sharding import PartitionSpec as P

HD = 64
PROMPT = 1024
CONT = 128
NCONT = 8
GROUP = 2048
BLOCK = 128

EPS_NORM = 1e-05
NEG_FILL = -1000000000.0
MESH = pl.DeviceIdType.MESH
F32 = jnp.float32
BF16 = jnp.bfloat16


def flip_low(r):
    return r + 1 - 2 * (r % 2)


def flip_high(r):
    return (r + 2) % 4


class Places:
    def __init__(self, ncol):
        self.dp = lax.axis_index("dp")
        self.row = lax.axis_index("row")
        self.col = lax.axis_index("col")
        self.ncol = ncol
        low, high = flip_low(self.row), flip_high(self.row)
        self.first = low * (1 - self.dp) + high * self.dp
        self.second = high * (1 - self.dp) + low * self.dp
        self.both = 3 - self.row
        self.sibling = (1 - self.dp, self.row, self.col)
        self.first_dev = (self.dp, self.first, self.col)
        self.second_dev = (self.dp, self.second, self.col)

    def ahead(self, k):
        return (self.col + k) % self.ncol

    def behind(self, k):
        return (self.col + self.ncol - k) % self.ncol

    def col_dev(self, c):
        return (self.dp, self.row, c)

    def meet(self):
        barrier = pltpu.get_barrier_semaphore()
        partners = [self.sibling, self.first_dev, self.second_dev]
        partners += [self.col_dev(self.ahead(k)) for k in range(1, self.ncol)]
        for partner in partners:
            pl.semaphore_signal(barrier, inc=1, device_id=partner, device_id_type=MESH)
        pl.semaphore_wait(barrier, len(partners))


def remote(src, dst, send_sem, recv_sem, device):
    return pltpu.make_async_remote_copy(
        src_ref=src,
        dst_ref=dst,
        send_sem=send_sem,
        recv_sem=recv_sem,
        device_id=device,
        device_id_type=MESH,
    )


def gather_kernel(
    ncol, parts, x_ref, td_ref, w_ref, xp_ref, xc_ref, tdo_ref, g_ref,
    act_send, act_recv, col_send, col_recv, one_send, one_recv, two_send, two_recv,
    sib_send, sib_recv, local_sem,
):
    at = Places(ncol)
    feat = x_ref.shape[0]
    half = feat // 2
    own_tokens = tdo_ref.shape[2]
    own_cont = xc_ref.shape[1]

    def rows_of(c):
        return pl.ds(pl.multiple_of(c * feat, feat), feat)

    def half_rows(c, core):
        return pl.ds(pl.multiple_of(c * feat + core * half, half), half)

    def prompt_cols(c):
        return pl.ds(pl.multiple_of(c // parts * GROUP, GROUP), PROMPT)

    def cont_cols(c):
        return pl.ds(
            pl.multiple_of(c // parts * GROUP + PROMPT + c % parts * own_cont, own_cont), own_cont
        )

    def own_cols(c):
        return pl.ds(pl.multiple_of(c * own_tokens, own_tokens), own_tokens)

    at.meet()
    my_half = w_ref.at[pl.ds(pl.multiple_of(at.dp * half, half), half)]
    pending = []

    def start(copy):
        copy.start()
        pending.append(copy)
        return copy

    mine = rows_of(at.col)
    for i, (src, dst) in enumerate(
        (
            (x_ref.at[:, prompt_cols(at.col)], xp_ref.at[mine]),
            (x_ref.at[:, cont_cols(at.col)], xc_ref.at[mine]),
            (td_ref.at[:, :, own_cols(at.col)], tdo_ref.at[:, mine]),
            (w_ref, g_ref.at[at.row, mine]),
        )
    ):
        pltpu.make_async_copy(src, dst, local_sem.at[i]).start()

    for k in range(1, ncol):
        start(
            remote(
                my_half,
                g_ref.at[at.row, half_rows(at.col, at.dp)],
                col_send.at[k],
                col_recv.at[k],
                at.col_dev(at.ahead(k)),
            )
        )
    for k in range(1, ncol):
        to = at.ahead(k)
        dev = at.col_dev(to)
        start(
            remote(
                x_ref.at[:, prompt_cols(to)], xp_ref.at[mine],
                act_send.at[0, k], act_recv.at[0, k], dev,
            )
        )
        start(
            remote(
                x_ref.at[:, cont_cols(to)], xc_ref.at[mine],
                act_send.at[1, k], act_recv.at[1, k], dev,
            )
        )
    for k in range(1, ncol):
        to = at.ahead(k)
        start(
            remote(
                td_ref.at[:, :, own_cols(to)], tdo_ref.at[:, mine],
                act_send.at[2, k], act_recv.at[2, k], at.col_dev(to),
            )
        )

    def piece(row, k, core):
        return g_ref.at[row, half_rows(at.behind(k), core)]

    def landed(dst, recv_sem):
        remote(dst, dst, recv_sem, recv_sem, at.sibling).wait_recv()

    def chunk(k):
        return my_half if k == 0 else piece(at.row, k, at.dp)

    for k in range(ncol):
        if k:
            landed(piece(at.row, k, at.dp), col_recv.at[k])
        start(remote(chunk(k), piece(at.row, k, at.dp), one_send.at[k], one_recv.at[k], at.first_dev))
        start(
            remote(chunk(k), piece(at.row, k, at.dp), two_send.at[0, k], two_recv.at[0, k], at.second_dev)
        )
        if k:
            start(
                remote(chunk(k), piece(at.row, k, at.dp), sib_send.at[0, k], sib_recv.at[0, k], at.sibling)
            )
    for k in range(ncol):
        got = piece(at.first, k, at.dp)
        landed(got, one_recv.at[k])
        start(remote(got, got, two_send.at[1, k], two_recv.at[1, k], at.second_dev))
        start(remote(got, got, sib_send.at[1, k], sib_recv.at[1, k], at.sibling))
    for k in range(ncol):
        for i, row in ((0, at.second), (1, at.both)):
            got = piece(row, k, at.dp)
            landed(got, two_recv.at[i, k])
            start(remote(got, got, sib_send.at[2 + i, k], sib_recv.at[2 + i, k], at.sibling))

    for k in range(1, ncol):
        frm = rows_of(at.behind(k))
        landed(xp_ref.at[frm], act_recv.at[0, k])
        landed(xc_ref.at[frm], act_recv.at[1, k])
        landed(tdo_ref.at[:, frm], act_recv.at[2, k])
    other = 1 - at.dp
    for k in range(ncol):
        if k:
            landed(piece(at.row, k, other), sib_recv.at[0, k])
        landed(piece(at.second, k, other), sib_recv.at[1, k])
        landed(piece(at.first, k, other), sib_recv.at[2, k])
        landed(piece(at.both, k, other), sib_recv.at[3, k])
    for copy in pending:
        copy.wait_send()
    for i, (src, dst) in enumerate(
        (
            (x_ref.at[:, prompt_cols(at.col)], xp_ref.at[mine]),
            (x_ref.at[:, cont_cols(at.col)], xc_ref.at[mine]),
            (td_ref.at[:, :, own_cols(at.col)], tdo_ref.at[:, mine]),
            (w_ref, g_ref.at[at.row, mine]),
        )
    ):
        pltpu.make_async_copy(src, dst, local_sem.at[i]).wait()


def gather_all(x_stream, teach_dy, packed, ncol, nrow, parts):
    feat = x_stream.shape[0]
    full = feat * ncol
    own_tokens = GROUP // parts
    own_cont = NCONT * CONT // parts
    dma = pltpu.SemaphoreType.DMA
    anywhere = pl.BlockSpec(memory_space=pl.ANY)
    return pl.pallas_call(
        functools.partial(gather_kernel, ncol, parts),
        out_shape=(
            jax.ShapeDtypeStruct((full, PROMPT), BF16),
            jax.ShapeDtypeStruct((full, own_cont), BF16),
            jax.ShapeDtypeStruct((2, full, own_tokens), BF16),
            jax.ShapeDtypeStruct((nrow, full, packed.shape[1]), BF16),
        ),
        in_specs=[anywhere] * 3,
        out_specs=[anywhere] * 4,
        scratch_shapes=[
            dma((3, ncol)), dma((3, ncol)), dma((ncol,)), dma((ncol,)), dma((ncol,)), dma((ncol,)),
            dma((2, ncol)), dma((2, ncol)), dma((4, ncol)), dma((4, ncol)), dma((4,)),
        ],
        compiler_params=pltpu.CompilerParams(collective_id=0, has_side_effects=True),
        name="gather_all",
    )(x_stream, teach_dy, packed)


def scatter_kernel(
    ncol, parts, xb_ref, gp_ref, gc_ref, gw_ref, sm_ref,
    xbo_ref, gpo_ref, gco_ref, gwo_ref, smo_ref,
    sib_buf, two_buf, one_buf, col_buf, sm_buf, smc_buf,
    act_send, act_recv, sib_send, sib_recv, two_send, two_recv, one_send, one_recv,
    col_send, col_recv, fin_send, fin_recv, sm_send, sm_recv, smc_send, smc_recv, local_sem,
):
    at = Places(ncol)
    feat = xbo_ref.shape[1]
    half = feat // 2
    own_tokens = xb_ref.shape[2]
    own_cont = gc_ref.shape[1]
    part = at.col % parts

    def rows_of(c):
        return pl.ds(pl.multiple_of(c * feat, feat), feat)

    def half_rows(c, core):
        return pl.ds(pl.multiple_of(c * feat + core * half, half), half)

    def prompt_cols(c):
        return pl.ds(pl.multiple_of(c // parts * PROMPT, PROMPT), PROMPT)

    def cont_cols(c):
        return pl.ds(pl.multiple_of(c * own_cont, own_cont), own_cont)

    def own_cols(c):
        return pl.ds(pl.multiple_of(c * own_tokens, own_tokens), own_tokens)

    at.meet()
    pending = []

    def start(copy):
        copy.start()
        pending.append(copy)
        return copy

    def landed(dst, recv_sem):
        remote(dst, dst, recv_sem, recv_sem, at.sibling).wait_recv()

    other = 1 - at.dp
    order = list(range(1, ncol)) + [0]
    for k in order:
        start(
            remote(
                gw_ref.at[:, half_rows(at.ahead(k), other)], sib_buf.at[k],
                sib_send.at[k], sib_recv.at[k], at.sibling,
            )
        )
    start(remote(sm_ref, sm_buf.at[0], sm_send.at[0], sm_recv.at[0], at.sibling))

    def local_copies():
        mine = rows_of(at.col)
        return [
            pltpu.make_async_copy(src, dst, local_sem.at[i])
            for i, (src, dst) in enumerate(
                (
                    (xb_ref.at[:, mine], xbo_ref.at[:, :, own_cols(at.col)]),
                    (gp_ref.at[mine], gpo_ref.at[part, :, prompt_cols(at.col)]),
                    (gc_ref.at[mine], gco_ref.at[:, cont_cols(at.col)]),
                )
            )
        ]

    for copy in local_copies():
        copy.start()
    for k in range(1, ncol):
        to = at.ahead(k)
        dev = at.col_dev(to)
        start(
            remote(
                xb_ref.at[:, rows_of(to)], xbo_ref.at[:, :, own_cols(at.col)],
                act_send.at[0, k], act_recv.at[0, k], dev,
            )
        )
        start(
            remote(
                gp_ref.at[rows_of(to)], gpo_ref.at[part, :, prompt_cols(at.col)],
                act_send.at[1, k], act_recv.at[1, k], dev,
            )
        )
        start(
            remote(
                gc_ref.at[rows_of(to)], gco_ref.at[:, cont_cols(at.col)],
                act_send.at[2, k], act_recv.at[2, k], dev,
            )
        )

    for k in order:
        landed(sib_buf.at[k], sib_recv.at[k])
        for row in range(gw_ref.shape[0]):
            here = gw_ref.at[row, half_rows(at.ahead(k), at.dp)]
            sib_buf[k, row] = (here[...].astype(F32) + sib_buf[k, row].astype(F32)).astype(BF16)
        for i, row in ((0, at.second), (1, at.both)):
            start(
                remote(
                    sib_buf.at[k, row], two_buf.at[i, k],
                    two_send.at[i, k], two_recv.at[i, k], at.second_dev,
                )
            )
    landed(sm_buf.at[0], sm_recv.at[0])
    sm_buf[3] = sm_ref[...] + sm_buf[0]
    start(remote(sm_buf.at[3], sm_buf.at[1], sm_send.at[1], sm_recv.at[1], at.second_dev))
    for k in order:
        landed(two_buf.at[1, k], two_recv.at[1, k])
        two_buf[1, k] = (sib_buf[k, at.first].astype(F32) + two_buf[1, k].astype(F32)).astype(BF16)
        start(
            remote(
                two_buf.at[1, k], one_buf.at[k], one_send.at[k], one_recv.at[k], at.first_dev
            )
        )
    landed(sm_buf.at[1], sm_recv.at[1])
    sm_buf[4] = sm_buf[3] + sm_buf[1]
    start(remote(sm_buf.at[4], sm_buf.at[2], sm_send.at[2], sm_recv.at[2], at.first_dev))
    for k in order:
        landed(two_buf.at[0, k], two_recv.at[0, k])
        landed(one_buf.at[k], one_recv.at[k])
        total = sib_buf[k, at.row].astype(F32) + two_buf[0, k].astype(F32) + one_buf[k].astype(F32)
        if k:
            two_buf[0, k] = total.astype(BF16)
            start(
                remote(
                    two_buf.at[0, k], col_buf.at[k],
                    col_send.at[k], col_recv.at[k], at.col_dev(at.ahead(k)),
                )
            )
        else:
            own_total = total
    landed(sm_buf.at[2], sm_recv.at[2])
    sm_buf[5] = sm_buf[4] + sm_buf[2]
    for k in range(1, ncol):
        to = at.ahead(k)
        start(
            remote(
                sm_buf.at[5, to], smc_buf.at[k], smc_send.at[k], smc_recv.at[k], at.col_dev(to)
            )
        )
    for k in range(1, ncol):
        landed(col_buf.at[k], col_recv.at[k])
        own_total = own_total + col_buf[k].astype(F32)
    my_rows = pl.ds(pl.multiple_of(at.dp * half, half), half)
    gwo_ref[my_rows] = own_total
    start(remote(gwo_ref.at[my_rows], gwo_ref.at[my_rows], fin_send, fin_recv, at.sibling))
    small = sm_buf[5, at.col]
    for k in range(1, ncol):
        landed(smc_buf.at[k], smc_recv.at[k])
        small = small + smc_buf[k]
    smo_ref[...] = small
    landed(gwo_ref.at[pl.ds(pl.multiple_of(other * half, half), half)], fin_recv)
    for k in range(1, ncol):
        frm = at.behind(k)
        landed(xbo_ref.at[:, :, own_cols(frm)], act_recv.at[0, k])
        landed(gpo_ref.at[frm % parts, :, prompt_cols(frm)], act_recv.at[1, k])
        landed(gco_ref.at[:, cont_cols(frm)], act_recv.at[2, k])
    for copy in pending:
        copy.wait_send()
    for copy in local_copies():
        copy.wait()


def scatter_all(xb, gp, gc, gw, small, ncol, parts):
    nrow, full, width = gw.shape
    feat = full // ncol
    half = feat // 2
    groups = ncol // parts
    own_tokens, own_cont = xb.shape[2], gc.shape[1]
    dma = pltpu.SemaphoreType.DMA
    anywhere = pl.BlockSpec(memory_space=pl.ANY)
    vmem = pl.BlockSpec(memory_space=pltpu.VMEM)
    small_shape = small.shape
    return pl.pallas_call(
        functools.partial(scatter_kernel, ncol, parts),
        out_shape=(
            jax.ShapeDtypeStruct((2, feat, ncol * own_tokens), BF16),
            jax.ShapeDtypeStruct((parts, feat, groups * PROMPT), BF16),
            jax.ShapeDtypeStruct((feat, ncol * own_cont), BF16),
            jax.ShapeDtypeStruct((feat, width), F32),
            jax.ShapeDtypeStruct(small_shape[1:], F32),
        ),
        in_specs=[anywhere, anywhere, anywhere, vmem, vmem],
        out_specs=[anywhere, anywhere, anywhere, vmem, vmem],
        scratch_shapes=[
            pltpu.VMEM((ncol, nrow, half, width), BF16),
            pltpu.VMEM((2, ncol, half, width), BF16),
            pltpu.VMEM((ncol, half, width), BF16),
            pltpu.VMEM((ncol, half, width), BF16),
            pltpu.VMEM((6,) + small_shape, F32),
            pltpu.VMEM((ncol,) + small_shape[1:], F32),
            dma((3, ncol)), dma((3, ncol)), dma((ncol,)), dma((ncol,)), dma((2, ncol)), dma((2, ncol)),
            dma((ncol,)), dma((ncol,)), dma((ncol,)), dma((ncol,)), dma(()), dma(()),
            dma((3,)), dma((3,)), dma((ncol,)), dma((ncol,)), dma((3,)),
        ],
        compiler_params=pltpu.CompilerParams(
            collective_id=1, has_side_effects=True, vmem_limit_bytes=56 << 20
        ),
        name="scatter_all",
    )(xb, gp, gc, gw, small)


def to_parts(array_in, parts):
    lead = array_in.shape[:-1]
    groups = array_in.shape[-1] // GROUP
    split = array_in.reshape(lead + (groups, GROUP))
    prompt = split[..., :PROMPT].reshape(lead + (groups, 2, parts, BLOCK))
    prompt = jnp.stack([prompt[..., 0, :, :], prompt[..., 1, ::-1, :]], axis=-2)
    prompt = prompt.reshape(lead + (groups, parts, PROMPT // parts))
    cont = split[..., PROMPT:].reshape(lead + (groups, parts, NCONT * CONT // parts))
    return jnp.concatenate([prompt, cont], axis=-1).reshape(array_in.shape)


def from_parts(array_in, parts):
    lead = array_in.shape[:-1]
    groups = array_in.shape[-1] // GROUP
    split = array_in.reshape(lead + (groups, parts, GROUP // parts))
    prompt = split[..., : PROMPT // parts].reshape(lead + (groups, parts, 2, BLOCK))
    prompt = jnp.concatenate(
        [prompt[..., :, 0, :], prompt[..., ::-1, 1, :]], axis=-2
    ).reshape(lead + (groups, PROMPT))
    cont = split[..., PROMPT // parts :].reshape(lead + (groups, NCONT * CONT))
    return jnp.concatenate([prompt, cont], axis=-1).reshape(array_in.shape)


def norm_forward(summed, gain_vec, bias_vec):
    average = jnp.mean(summed, axis=0, keepdims=True)
    squares = jnp.mean(summed * summed, axis=0, keepdims=True)
    inv_scale = lax.rsqrt(squares - average * average + EPS_NORM)
    unit_val = (summed - average) * inv_scale
    return (unit_val * gain_vec + bias_vec, unit_val, inv_scale)


def norm_backward(upstream, unit_val, inv_scale, gain_vec):
    scaled = upstream * gain_vec
    first = jnp.mean(scaled, axis=0, keepdims=True)
    second = jnp.mean(scaled * unit_val, axis=0, keepdims=True)
    d_summed = inv_scale * (scaled - first - unit_val * second)
    sums = [jnp.sum(v, axis=1, keepdims=True) for v in (upstream * unit_val, upstream)]
    return (d_summed, *sums)


def dot_tn(lhs, rhs):
    return lax.dot_general(lhs, rhs, (((0,), (0,)), ((), ())), preferred_element_type=F32)


def dot_nn(lhs, rhs):
    return lax.dot_general(lhs, rhs, (((1,), (0,)), ((), ())), preferred_element_type=F32)


def dot_nt(lhs, rhs):
    return lax.dot_general(lhs, rhs, (((1,), (1,)), ((), ())), preferred_element_type=F32)


def iota(shape, axis):
    return lax.broadcasted_iota(jnp.int32, shape, axis)


def fold(array_in, op):
    return op(array_in.reshape(array_in.shape[0] // 8, 8, array_in.shape[1]), axis=0)


KEYS = 256
PAIR = 2 * BLOCK


class Layer:
    def __init__(self, part, parts, lens, total_tokens, count):
        self.part, self.parts = part, parts
        self.lens = lens
        self.total_tokens, self.count = total_tokens, count
        slot = iota((1, BLOCK), 1)
        low, high = part * BLOCK + slot, (2 * parts - 1 - part) * BLOCK + slot
        last = lens[0] - 1
        self.bound = jnp.concatenate(
            [jnp.minimum(low, last), jnp.minimum(high, last), jnp.full((1, PAIR), last, jnp.int32)],
            axis=1,
        )
        live = [low < lens[0], high < lens[0]] + [slot < n for n in lens[1:]]
        self.live = jnp.concatenate([m.astype(F32) for m in live], axis=1)

    def own_columns(self):
        low = pl.ds(pl.multiple_of(self.part * BLOCK, BLOCK), BLOCK)
        high = pl.ds(pl.multiple_of((2 * self.parts - 1 - self.part) * BLOCK, BLOCK), BLOCK)
        return low, high

    def project(self, xp, xc, w, xo, xt, kv, kvt, qt):
        low, high = self.own_columns()
        xo[:, :BLOCK] = xp[:, low]
        xo[:, BLOCK:PAIR] = xp[:, high]
        xo[:, PAIR:] = xc[...]
        xt[:PROMPT] = xp[...].T
        xt[PROMPT:] = xc[...].T

        def step(r, carry):
            wq, wkv = w[r, :, :BLOCK], w[r, :, BLOCK : 3 * BLOCK]
            cols = pl.ds(pl.multiple_of(r * PAIR, PAIR), PAIR)
            kv[:, cols] = dot_nn(xt[...], wkv).astype(BF16)
            kvt[r, :, :PROMPT] = dot_tn(wkv, xp[...]).astype(BF16)
            kvt[r, :, PROMPT:] = dot_tn(wkv, xc[...]).astype(BF16)
            rows = pl.ds(pl.multiple_of(r * BLOCK, BLOCK), BLOCK)
            qt[rows] = (dot_tn(wq, xo[...]).astype(BF16).astype(F32) * HD ** (-0.5)).astype(BF16)
            return carry

        lax.fori_loop(0, w.shape[0], step, 0)

    def one_head(self, array_in, head):
        zeros = jnp.zeros((HD, array_in.shape[1]), array_in.dtype)
        mine = array_in[head * HD : (head + 1) * HD]
        return jnp.concatenate([mine, zeros] if head == 0 else [zeros, mine], axis=0)

    def masked(self, score, first_key, columns):
        keys = iota(score.shape, 0) + first_key
        return jnp.where(keys <= self.bound[:, columns], score, NEG_FILL)

    def masked_own(self, score, n):
        keys = iota(score.shape, 0)
        return jnp.where(
            (keys <= iota(score.shape, 1)) & (keys < self.lens[1 + n]), score, NEG_FILL
        )

    def attend(self, kv, kvt, qt, att, lse, s_scr, p_scr):
        def step(r, carry):
            k_cols = pl.ds(pl.multiple_of(r * PAIR, PAIR), BLOCK)
            q_pair = qt[pl.ds(pl.multiple_of(r * BLOCK, BLOCK), BLOCK)]
            for head in range(2):
                query = self.one_head(q_pair, head)
                v_rows = slice(BLOCK + head * HD, BLOCK + (head + 1) * HD)
                for b in range(2):
                    columns = slice(b * PAIR, (b + 1) * PAIR)
                    q_here = query[:, columns]
                    top = jnp.full((8, PAIR), NEG_FILL, F32)
                    for first in range(0, PROMPT, KEYS):
                        score = dot_nn(kv[first : first + KEYS, k_cols], q_here)
                        score = self.masked(score, first, columns)
                        s_scr[head, first : first + KEYS] = score
                        top = jnp.maximum(top, fold(score, jnp.max))
                    own_scores = []
                    if b == 1:
                        for n in range(2):
                            keys = slice(PROMPT + n * BLOCK, PROMPT + (n + 1) * BLOCK)
                            score = dot_nn(kv[keys, k_cols], q_here[:, n * BLOCK : (n + 1) * BLOCK])
                            own_scores.append(self.masked_own(score, n))
                        own_top = [fold(score, jnp.max) for score in own_scores]
                        top = jnp.maximum(top, jnp.concatenate(own_top, axis=1))
                    top = jnp.max(top, axis=0, keepdims=True)
                    total = jnp.zeros((8, PAIR), F32)
                    for first in range(0, PROMPT, KEYS):
                        prob = jnp.exp(s_scr[head, first : first + KEYS] - top)
                        total = total + fold(prob, jnp.sum)
                        p_scr[head, first : first + KEYS] = prob.astype(BF16)
                    out = dot_nn(kvt[r, v_rows, :PROMPT], p_scr[head])
                    if b == 1:
                        own_out, own_total = [], []
                        for n in range(2):
                            lanes = slice(n * BLOCK, (n + 1) * BLOCK)
                            prob = jnp.exp(own_scores[n] - top[:, lanes])
                            own_total.append(fold(prob, jnp.sum))
                            keys = slice(PROMPT + n * BLOCK, PROMPT + (n + 1) * BLOCK)
                            own_out.append(dot_nn(kvt[r, v_rows, keys], prob.astype(BF16)))
                        total = total + jnp.concatenate(own_total, axis=1)
                        out = out + jnp.concatenate(own_out, axis=1)
                    total = jnp.sum(total, axis=0, keepdims=True)
                    rows = pl.ds(pl.multiple_of(r * BLOCK + head * HD, HD), HD)
                    att[rows, columns] = (out / total).astype(BF16)
                    lse[pl.ds(2 * r + head, 1), columns] = top + jnp.log(total)
            return carry

        lax.fori_loop(0, kvt.shape[0], step, 0)

    def attend_back(self, kv, kvt, qt, lse, delta, d_att, dkvt, dqt, p_scr, ds_scr):
        def step(r, carry):
            k_cols = pl.ds(pl.multiple_of(r * PAIR, PAIR), BLOCK)
            v_cols = pl.ds(pl.multiple_of(r * PAIR + BLOCK, BLOCK), BLOCK)
            pair = pl.ds(pl.multiple_of(r * BLOCK, BLOCK), BLOCK)
            q_pair, d_pair = qt[pair], d_att[pair]
            for head in range(2):
                query, d_out = self.one_head(q_pair, head), self.one_head(d_pair, head)
                q_mine = q_pair[head * HD : (head + 1) * HD]
                d_mine = d_pair[head * HD : (head + 1) * HD]
                k_rows = slice(head * HD, (head + 1) * HD)
                v_rows = slice(BLOCK + head * HD, BLOCK + (head + 1) * HD)
                norm = lse[pl.ds(2 * r + head, 1)]
                dlt = delta[pl.ds(2 * r + head, 1)]
                for b in range(2):
                    columns = slice(b * PAIR, (b + 1) * PAIR)
                    for first in range(0, PROMPT, KEYS):
                        keys = slice(first, first + KEYS)
                        score = dot_nn(kv[keys, k_cols], query[:, columns])
                        score = self.masked(score, first, columns)
                        prob = jnp.exp(score - norm[:, columns])
                        dprob = dot_nn(kv[keys, v_cols], d_out[:, columns])
                        p_scr[head, keys, columns] = prob.astype(BF16)
                        ds_scr[head, keys, columns] = (prob * (dprob - dlt[:, columns])).astype(BF16)
                d_query = dot_nn(kvt[r, k_rows, :PROMPT], ds_scr[head])
                own_dq = [jnp.zeros((HD, PAIR), F32)]
                for n in range(2):
                    keys = slice(PROMPT + n * BLOCK, PROMPT + (n + 1) * BLOCK)
                    lanes = slice(PAIR + n * BLOCK, PAIR + (n + 1) * BLOCK)
                    score = self.masked_own(dot_nn(kv[keys, k_cols], query[:, lanes]), n)
                    prob = jnp.exp(score - norm[:, lanes])
                    dprob = dot_nn(kv[keys, v_cols], d_out[:, lanes])
                    d_score = (prob * (dprob - dlt[:, lanes])).astype(BF16)
                    own_dq.append(dot_nn(kvt[r, k_rows, keys], d_score))
                    dkvt[r, k_rows, keys] = dot_nt(q_mine[:, lanes], d_score).astype(BF16)
                    dkvt[r, v_rows, keys] = dot_nt(d_mine[:, lanes], prob.astype(BF16)).astype(BF16)
                d_query = (d_query + jnp.concatenate(own_dq, axis=1)) * HD ** (-0.5)
                rows = pl.ds(pl.multiple_of(r * BLOCK + head * HD, HD), HD)
                dqt[rows] = d_query.astype(BF16)
                dkvt[r, k_rows, :PROMPT] = dot_nt(q_mine, ds_scr[head]).astype(BF16)
                dkvt[r, v_rows, :PROMPT] = dot_nt(d_mine, p_scr[head]).astype(BF16)
            return carry

        lax.fori_loop(0, kvt.shape[0], step, 0)

    def input_grads(self, xp, xc, xo, w, dkvt, dqt, dsa, gp, gc, gw, dx, dxo):
        for r in range(w.shape[0]):
            wq, wkv = w[r, :, :BLOCK], w[r, :, BLOCK : 3 * BLOCK]
            part = dot_nn(wkv, dkvt[r])
            rows = slice(r * BLOCK, (r + 1) * BLOCK)
            own = dot_nn(wq, dqt[rows])
            if r == 0:
                dx[...] = part
                dxo[...] = dsa[...] + own
            else:
                dx[...] += part
                dxo[...] += own
            gw[r, :, :BLOCK] = dot_nt(xo[...], dqt[rows]).astype(BF16)
            gw[r, :, BLOCK : 3 * BLOCK] = (
                dot_nt(xp[...], dkvt[r, :, :PROMPT]) + dot_nt(xc[...], dkvt[r, :, PROMPT:])
            ).astype(BF16)
        low, high = self.own_columns()
        dx[:, low] += dxo[:, :BLOCK]
        dx[:, high] += dxo[:, BLOCK:PAIR]
        gp[...] = dx[:, :PROMPT].astype(BF16)
        gc[...] = (dx[:, PROMPT:] + dxo[:, PAIR:]).astype(BF16)

    def middle(self, xo, tdo, w, vec, att, xb, gw, sm, d_att, delta, dsa, hid, acc, ba):
        nrow, full = w.shape[0], w.shape[1]
        ff = (w.shape[2] - 4 * BLOCK) // 2
        up, down = slice(4 * BLOCK, 4 * BLOCK + ff), slice(4 * BLOCK + ff, 4 * BLOCK + 2 * ff)
        gain_a, bias_a, gain_f, bias_f = (vec[:, i : i + 1].astype(F32) for i in range(4))
        w_o = jnp.concatenate([w[r, :, 3 * BLOCK : 4 * BLOCK] for r in range(nrow)], axis=1)
        ba[...] = dot_nn(w_o, att[...])
        x_one, unit_a, inv_a = norm_forward(xo[...].astype(F32) + ba[...], gain_a, bias_a)
        x_low = x_one.astype(BF16)
        x_low_t = x_low.T
        acc[...] = jnp.zeros_like(acc)

        def up_down(r, carry):
            pre = dot_nn(x_low_t, w[r, :, up])
            hidden = jnp.maximum(pre, 0.0).astype(BF16)
            hid[r] = hidden
            acc[...] += dot_nt(w[r, :, down], hidden)
            return carry

        lax.fori_loop(0, nrow, up_down, 0)
        branch_f = acc[...]
        x_two, unit_f, inv_f = norm_forward(x_one + branch_f, gain_f, bias_f)
        branch = ba[...] + branch_f
        xb[0] = x_two.astype(BF16)
        xb[1] = branch.astype(BF16)
        diff_x = x_two - tdo[0].astype(F32)
        diff_y = branch + tdo[1].astype(F32)
        loss = jnp.sum(self.live * (diff_x * diff_x + diff_y * diff_y))
        weight = self.live * (self.total_tokens / self.count)
        grad_y = diff_y * weight
        d_sum_f, gain_grad_f, bias_grad_f = norm_backward(diff_x * weight, unit_f, inv_f, gain_f)
        d_branch_f = (d_sum_f + grad_y).astype(BF16)
        d_branch_t = d_branch_f.T
        acc[...] = d_sum_f

        def back(r, carry):
            hidden = hid[r]
            d_hidden = dot_nn(d_branch_t, w[r, :, down])
            d_pre = jnp.where(hidden.astype(F32) > 0, d_hidden, 0.0).astype(BF16)
            gw[r, :, up] = dot_nn(x_low, d_pre).astype(BF16)
            gw[r, :, down] = dot_nn(d_branch_f, hidden).astype(BF16)
            acc[...] += dot_nt(w[r, :, up], d_pre)
            return carry

        lax.fori_loop(0, nrow, back, 0)
        d_sum_a, gain_grad_a, bias_grad_a = norm_backward(acc[...], unit_a, inv_a, gain_a)
        dsa[...] = d_sum_a
        d_branch_a = (d_sum_a + grad_y).astype(BF16)
        for r in range(nrow):
            rows = slice(r * BLOCK, (r + 1) * BLOCK)
            attended = att[rows]
            gw[r, :, 3 * BLOCK : 4 * BLOCK] = dot_nt(d_branch_a, attended).astype(BF16)
            d_here = dot_tn(w[r, :, 3 * BLOCK : 4 * BLOCK], d_branch_a).astype(BF16)
            d_att[rows] = d_here
            product = attended.astype(F32) * d_here.astype(F32)
            for head in range(2):
                delta[2 * r + head : 2 * r + head + 1] = jnp.sum(
                    product[head * HD : (head + 1) * HD], axis=0, keepdims=True
                )
        lane = iota((full, 128), 1)
        sums = jnp.zeros((full, 128), F32)
        for i, vector in enumerate((gain_grad_a, bias_grad_a, gain_grad_f, bias_grad_f)):
            sums = jnp.where(lane == i, vector, sums)
        sums = jnp.where(lane == 4, loss, sums)
        sm[...] = sums.T[:8]


def layer_kernel(
    parts, lens_ref, len_table, xp, xc, tdo, w, vec, xb, gp, gc, gw, sm,
    xo, xt, kv, kvt, qt, att, lse, delta, d_att, dkvt, dqt, s_scr, pf_scr, p_scr, ds_scr,
    dsa, hid, acc, ba, dx,
):
    col = lax.axis_index("col")
    groups = lax.axis_size("col") // parts
    chip = lax.axis_index("dp") * lax.axis_size("row") + lax.axis_index("row")
    group = chip * groups + col // parts
    part = col % parts
    lens = [lens_ref[group, 0]] + [lens_ref[group, 1 + 2 * part + n] for n in range(2)]
    count = jnp.sum(len_table[...].astype(F32))
    layer = Layer(part, parts, lens, lens_ref.shape[0] * GROUP, count)
    layer.project(xp, xc, w, xo, xt, kv, kvt, qt)
    layer.attend(kv, kvt, qt, att, lse, s_scr, pf_scr)
    layer.middle(xo, tdo, w, vec, att, xb, gw, sm, d_att, delta, dsa, hid, acc, ba)
    layer.attend_back(kv, kvt, qt, lse, delta, d_att, dkvt, dqt, p_scr, ds_scr)
    layer.input_grads(xp, xc, xo, w, dkvt, dqt, dsa, gp, gc, gw, dx, acc)


def run_layer(lengths, xp, xc, tdo, weights, vec, parts):
    nrow, full, width = weights.shape
    own, keys = tdo.shape[2], xp.shape[1] + xc.shape[1]
    heads = full // HD
    vmem = pl.BlockSpec(memory_space=pltpu.VMEM)
    return pl.pallas_call(
        functools.partial(layer_kernel, parts),
        out_shape=(
            jax.ShapeDtypeStruct((2, full, own), BF16),
            jax.ShapeDtypeStruct(xp.shape, BF16),
            jax.ShapeDtypeStruct(xc.shape, BF16),
            jax.ShapeDtypeStruct(weights.shape, BF16),
            jax.ShapeDtypeStruct((8, full), F32),
        ),
        in_specs=[pl.BlockSpec(memory_space=pltpu.SMEM)] + [vmem] * 6,
        out_specs=[vmem] * 5,
        scratch_shapes=[
            pltpu.VMEM((full, own), BF16),
            pltpu.VMEM((keys, full), BF16),
            pltpu.VMEM((keys, nrow * PAIR), BF16),
            pltpu.VMEM((nrow, PAIR, keys), BF16),
            pltpu.VMEM((full, own), BF16),
            pltpu.VMEM((full, own), BF16),
            pltpu.VMEM((heads, own), F32),
            pltpu.VMEM((heads, own), F32),
            pltpu.VMEM((full, own), BF16),
            pltpu.VMEM((nrow, PAIR, keys), BF16),
            pltpu.VMEM((full, own), BF16),
            pltpu.VMEM((2, PROMPT, PAIR), F32),
            pltpu.VMEM((2, PROMPT, PAIR), BF16),
            pltpu.VMEM((2, PROMPT, own), BF16),
            pltpu.VMEM((2, PROMPT, own), BF16),
            pltpu.VMEM((full, own), F32),
            pltpu.VMEM((nrow, own, (width - 4 * BLOCK) // 2), BF16),
            pltpu.VMEM((full, own), F32),
            pltpu.VMEM((full, own), F32),
            pltpu.VMEM((full, keys), F32),
        ],
        compiler_params=pltpu.CompilerParams(vmem_limit_bytes=60 << 20),
        name="layer",
    )(lengths, lengths, xp, xc, tdo, weights, vec)


def body(
    x_stream, y_stream, w_qkv, w_out, gain_attn, bias_attn, w_up, w_down, gain_ffn, bias_ffn,
    teach_x, teach_y, lengths,
):
    ncol, nrow = lax.axis_size("col"), lax.axis_size("row")
    feat, tokens = x_stream.shape
    full = feat * ncol
    groups_here = tokens // GROUP
    parts = ncol // groups_here
    assert parts * 2 * BLOCK == PROMPT and nrow == 4
    block = w_qkv.shape[2]
    ff_block = w_up.shape[1]

    y_f32 = y_stream.astype(F32)
    dy = y_f32 - teach_y.astype(F32)
    teach_dy = to_parts(jnp.stack([teach_x, dy.astype(BF16)]), parts)
    packed = jnp.concatenate([w_qkv.reshape(feat, 3 * block), w_out.T, w_up, w_down.T], axis=1)
    small_vecs = jnp.stack([gain_attn, bias_attn, gain_ffn, bias_ffn])
    vecs = lax.all_gather(small_vecs, "col", axis=1, tiled=True)

    x_prompt, x_cont, tdo, weights = gather_all(x_stream, teach_dy, packed, ncol, nrow, parts)

    first = (lax.axis_index("dp") * nrow + lax.axis_index("row")) * groups_here
    count_all = jnp.sum(lengths).astype(F32)
    total_tokens = lengths.shape[0] * GROUP
    vec = jnp.pad(vecs.T, ((0, 0), (0, 124)))
    xb, gp, gc, gw, small = run_layer(lengths, x_prompt, x_cont, tdo, weights, vec, parts)
    lanes = max(feat, 128)
    small = small.reshape(8, ncol, feat).transpose(1, 0, 2)
    small = jnp.pad(small, ((0, 0), (0, 0), (0, lanes - feat)))
    xb, gp, gc, gw, sums = scatter_all(xb, gp, gc, gw, small, ncol, parts)

    xb = from_parts(xb, parts)
    branch = xb[1].astype(F32)
    live_all = live_slots(
        lax.dynamic_slice_in_dim(lengths, first, groups_here, 0)
    ).reshape(1, tokens)
    y_out = (y_f32 + branch).astype(BF16)
    grad_y_out = (dy + branch) * (live_all * (total_tokens / count_all))
    gp = jnp.sum(gp.astype(F32), axis=0).reshape(feat, groups_here, PROMPT)
    gc = gc.astype(F32).reshape(feat, groups_here, NCONT * CONT)
    grad_x = jnp.concatenate([gp, gc], axis=2).reshape(feat, tokens)
    loss = sums[4, 0] / (2.0 * count_all * full)
    first_up = 4 * block
    return (
        xb[0],
        y_out,
        grad_x,
        grad_y_out,
        gw[:, : 3 * block].reshape(feat, 3, block),
        gw[:, 3 * block : 4 * block].T,
        sums[0, :feat],
        sums[1, :feat],
        gw[:, first_up : first_up + ff_block],
        gw[:, first_up + ff_block :].T,
        sums[2, :feat],
        sums[3, :feat],
        loss,
    )


def live_slots(lens):
    prompt = jnp.arange(PROMPT, dtype=jnp.int32)[None, :] < lens[:, 0:1]
    cont = jnp.arange(CONT, dtype=jnp.int32)[None, None, :] < lens[:, 1:, None]
    cont = cont.reshape(lens.shape[0], NCONT * CONT)
    return jnp.concatenate([prompt, cont], axis=1).astype(F32)


def solution(mesh):
    stream = P("col", ("dp", "row"))
    up, down = P("col", "row"), P("row", "col")
    qkv, vec = P("col", None, "row"), P("col")
    return jax.shard_map(
        body,
        mesh=mesh,
        in_specs=(
            stream, stream, qkv, down, vec, vec, up, down, vec, vec, stream, stream, P(),
        ),
        out_specs=(
            stream, stream, stream, stream, qkv, down, vec, vec, up, down, vec, vec, P(),
        ),
        check_vma=False,
    )
```

profile of v0, /device:TPU:13, one launch (start us, length us, event | category | flops | bytes accessed | tf_op | source)
XLA Modules:
  0.0 238.9 jit_solution(8304208649479899137)
XLA Ops:
  0.6 1.3 fusion.3
  2.0 1.1 maximum_bitcast_fusion
  3.8 0.5 rev.6
  5.5 1.6 reshape.127.td_ref
  7.6 0.8 pad_maximum_fusion.2.w_ref
  8.4 71.6 %gather_all.1 = (bf16[512,1024]{1,0:T(8,128)(2,1)}, bf16[512,256]{1,0:T(8,128)(2,1)}, bf16[2,512,512]{2,1,0:T(8,128)(2,1)}, bf16[4,512,1536]{2,1,0:T(8,128)(2,1)}) custom-call(bf16[128,2048]{1,0:T(8,128)(2,1)} %x_ref.1, bf16[2,128,2048]{2,1,0:T(8,128)(2,1)} %reshape.127.td_ref, bf16[128,1536]{1,0:T(8,128)(2,1)} %pad_maximum_fusion.2.w_ref), custom_call_target="tpu_custom_call" | custom-call | tf_op jit(solution)/shard_map/gather_all/pallas_call | solution.py:220
  80.3 10.5 %all_gather.3 = bf16[4,512]{0,1:T(8,128)(2,1)S(1)} all-gather(bf16[4,128]{0,1:T(8,128)(2,1)S(1)} %copy.62), channel_id=1, replica_groups=mesh['dp'=2,'row'=4,'col'=4] {'col'}, dimensions={1}, use_global_device_ids=true | all-gather | bytes 5120 | tf_op jit(solution)/shard_map/all_gather | solution.py:821
  90.7 0.7 pad.4.vec
  91.4 51.3 %layer.1 = (bf16[2,512,512]{2,1,0:T(8,128)(2,1)}, bf16[512,1024]{1,0:T(8,128)(2,1)}, bf16[512,256]{1,0:T(8,128)(2,1)}, bf16[4,512,1536]{2,1,0:T(8,128)(2,1)}, f32[8,512]{1,0:T(8,128)}) custom-call(s32[8,9]{1,0:T(8,128)} %len_table.1, s32[8,9]{1,0:T(8,128)} %len_table.1, bf16[512,1024]{1,0:T(8,128)(2,1)} %get-tuple-element.27.xp, ...), custom_call_target="tpu_custom_call" | custom-call | tf_op jit(solution)/shard_map/layer/pallas_call | solution.py:765
  142.8 78.7 %scatter_all.1 = (bf16[2,128,2048]{2,1,0:T(8,128)(2,1)}, bf16[4,128,1024]{2,1,0:T(8,128)(2,1)}, bf16[128,1024]{1,0:T(8,128)(2,1)}, f32[128,1536]{1,0:T(8,128)}, f32[8,128]{1,0:T(8,128)}) custom-call(bf16[2,512,512]{2,1,0:T(8,128)(2,1)} %get-tuple-element.31.xb_ref, bf16[512,1024]{1,0:T(8,128)(2,1)} %get-tuple-element.32.gp_ref, ...), custom_call_target="tpu_custom_call" | custom-call | tf_op jit(solution)/shard_map/scatter_all/pallas_call | solution.py:409
  221.5 1.5 convert_reduce_fusion
  223.0 1.0 bitcast_convert_fusion
  224.0 1.0 maximum_bitcast_fusion.1
  225.0 0.8 reshape.130
  226.4 0.7 fusion.6
  227.2 0.5 rev.7
  229.1 0.6 reduce_sum.19
  230.5 1.4 fusion.1
  231.9 0.8 slice_bitcast_fusion.1
  232.8 0.7 slice_bitcast_fusion.3
  233.5 0.8 copy.68
  234.5 0.8 copy.66
  235.3 0.7 copy.67
  237.2 0.5 slice_bitcast_fusion.5
  (58 shorter events, 5.0 us)
Async XLA Ops:
  5.0 2.1 copy-start.6
  5.0 2.4 copy-start.4
  5.0 2.5 %copy-start.8 = (bf16[128,128]{1,0:T(8,128)(2,1)S(1)}, bf16[128,128]{1,0:T(8,128)(2,1)}, u32[]{:S(2)}) copy-start(bf16[128,128]{1,0:T(8,128)(2,1)} %param.16) | copy-start | bytes 98308
  5.0 2.6 %copy-start.5 = (bf16[128,512]{1,0:T(8,128)(2,1)S(1)}, bf16[128,512]{1,0:T(8,128)(2,1)}, u32[]{:S(2)}) copy-start(bf16[128,512]{1,0:T(8,128)(2,1)} %param.19) | copy-start | bytes 393220
  7.1 73.0 %copy-start.10 = (bf16[128]{0:T(256)(128)(2,1)S(1)}, bf16[128]{0:T(256)(128)(2,1)}, u32[]{:S(2)}) copy-start(bf16[128]{0:T(256)(128)(2,1)} %param.22) | copy-start | bytes 772
  7.1 73.0 %copy-start.11 = (bf16[128]{0:T(256)(128)(2,1)S(1)}, bf16[128]{0:T(256)(128)(2,1)}, u32[]{:S(2)}) copy-start(bf16[128]{0:T(256)(128)(2,1)} %param.21) | copy-start | bytes 772
  7.1 73.0 %copy-start.12 = (bf16[128]{0:T(256)(128)(2,1)S(1)}, bf16[128]{0:T(256)(128)(2,1)}, u32[]{:S(2)}) copy-start(bf16[128]{0:T(256)(128)(2,1)} %param.18) | copy-start | bytes 772
  7.1 73.0 %copy-start.13 = (bf16[128]{0:T(256)(128)(2,1)S(1)}, bf16[128]{0:T(256)(128)(2,1)}, u32[]{:S(2)}) copy-start(bf16[128]{0:T(256)(128)(2,1)} %param.17) | copy-start | bytes 772
  221.4 3.6 %copy-start.2 = (bf16[2,128,2048]{2,1,0:T(8,128)(2,1)S(1)}, bf16[2,128,2048]{2,1,0:T(8,128)(2,1)}, u32[]{:S(2)}) copy-start(bf16[2,128,2048]{2,1,0:T(8,128)(2,1)} %get-tuple-element.36) | copy-start | bytes 3145732
  228.2 0.7 copy-start.7
  228.2 2.3 copy-start
  228.2 2.3 copy-start.1
  230.5 2.3 copy-start.3
  231.9 4.1 %copy-start.9 = (f32[8,128]{1,0:T(8,128)S(1)}, f32[8,128]{1,0:T(8,128)}, u32[]{:S(2)}) copy-start(f32[8,128]{1,0:T(8,128)} %get-tuple-element.40) | copy-start | bytes 12292
where the time goes:
time: 240 us; the launch traced here: 239 us
  Pallas kernels  202 us (84%)
  local copies, waits for them, and re-layouts  13.2 us (6%)
  blocking collectives  10.5 us (4%)
  other arithmetic  9.96 us (4%)
  between operations  3.55 us (1%)
    pallas_call x1, Pallas kernels, scatter_all(): pl.pallas_call(functools.partial(scatter_kernel, ncol, parts), out_shape=...  78.7 us
    pallas_call x1, Pallas kernels, gather_all(): pl.pallas_call(functools.partial(gather_kernel, ncol, parts), out_shape=(...  71.6 us
    pallas_call x1, Pallas kernels, run_layer(): pl.pallas_call(functools.partial(layer_kernel, parts), out_shape=(jax.Sha...  51.3 us
    all_gather x1, blocking collectives, body(): vecs = lax.all_gather(small_vecs, 'col', axis=1, tiled=True)  10.5 us

commit v1 on v0

--- a/solution.py
+++ b/solution.py
@@ -42,12 +42,14 @@
         self.sibling = (1 - self.dp, self.row, self.col)
         self.first_dev = (self.dp, self.first, self.col)
         self.second_dev = (self.dp, self.second, self.col)
+        self.aheads = [(self.col + k) % ncol for k in range(ncol)]
+        self.behinds = [(self.col + ncol - k) % ncol for k in range(ncol)]
 
     def ahead(self, k):
-        return (self.col + k) % self.ncol
+        return self.aheads[k]
 
     def behind(self, k):
-        return (self.col + self.ncol - k) % self.ncol
+        return self.behinds[k]
 
     def col_dev(self, c):
         return (self.dp, self.row, c)
@@ -554,7 +556,7 @@
             (keys <= iota(score.shape, 1)) & (keys < self.lens[1 + n]), score, NEG_FILL
         )
 
-    def attend(self, kv, kvt, qt, att, lse, s_scr, p_scr):
+    def attend(self, kv, kvt, qt, att, lse, s_scr, p_scr, between=None):
         def step(r, carry):
             k_cols = pl.ds(pl.multiple_of(r * PAIR, PAIR), BLOCK)
             q_pair = qt[pl.ds(pl.multiple_of(r * BLOCK, BLOCK), BLOCK)]
@@ -599,11 +601,15 @@
                     rows = pl.ds(pl.multiple_of(r * BLOCK + head * HD, HD), HD)
                     att[rows, columns] = (out / total).astype(BF16)
                     lse[pl.ds(2 * r + head, 1), columns] = top + jnp.log(total)
+            if between is not None:
+                between(r)
             return carry
 
         lax.fori_loop(0, kvt.shape[0], step, 0)
 
-    def attend_back(self, kv, kvt, qt, lse, delta, d_att, dkvt, dqt, p_scr, ds_scr):
+    def attend_back(
+        self, kv, kvt, qt, lse, delta, d_att, dkvt, dqt, p_scr, ds_scr, between=None, grads=None
+    ):
         def step(r, carry):
             k_cols = pl.ds(pl.multiple_of(r * PAIR, PAIR), BLOCK)
             v_cols = pl.ds(pl.multiple_of(r * PAIR + BLOCK, BLOCK), BLOCK)
@@ -644,9 +650,19 @@
                 dqt[rows] = d_query.astype(BF16)
                 dkvt[r, k_rows, :PROMPT] = dot_nt(q_mine, ds_scr[head]).astype(BF16)
                 dkvt[r, v_rows, :PROMPT] = dot_nt(d_mine, p_scr[head]).astype(BF16)
+            if grads is not None:
+                self.projection_grads(r, pair, *grads, dkvt, dqt)
+            if between is not None:
+                between(r)
             return carry
 
         lax.fori_loop(0, kvt.shape[0], step, 0)
+
+    def projection_grads(self, r, rows, xp, xc, xo, gw, dkvt, dqt):
+        gw[r, :, :BLOCK] = dot_nt(xo[...], dqt[rows]).astype(BF16)
+        gw[r, :, BLOCK : 3 * BLOCK] = (
+            dot_nt(xp[...], dkvt[r, :, :PROMPT]) + dot_nt(xc[...], dkvt[r, :, PROMPT:])
+        ).astype(BF16)
 
     def input_grads(self, xp, xc, xo, w, dkvt, dqt, dsa, gp, gc, gw, dx, dxo):
         for r in range(w.shape[0]):
@@ -660,17 +676,17 @@
             else:
                 dx[...] += part
                 dxo[...] += own
-            gw[r, :, :BLOCK] = dot_nt(xo[...], dqt[rows]).astype(BF16)
-            gw[r, :, BLOCK : 3 * BLOCK] = (
-                dot_nt(xp[...], dkvt[r, :, :PROMPT]) + dot_nt(xc[...], dkvt[r, :, PROMPT:])
-            ).astype(BF16)
+            self.projection_grads(r, rows, xp, xc, xo, gw, dkvt, dqt)
         low, high = self.own_columns()
         dx[:, low] += dxo[:, :BLOCK]
         dx[:, high] += dxo[:, BLOCK:PAIR]
         gp[...] = dx[:, :PROMPT].astype(BF16)
         gc[...] = (dx[:, PROMPT:] + dxo[:, PAIR:]).astype(BF16)
 
-    def middle(self, xo, tdo, w, vec, att, xb, gw, sm, d_att, delta, dsa, hid, acc, ba):
+    def middle(
+        self, xo, tdo, w, vec, att, xb, gw, sm, d_att, delta, dsa, hid, acc, ba,
+        tokens_ready=None, outputs_ready=None,
+    ):
         nrow, full = w.shape[0], w.shape[1]
         ff = (w.shape[2] - 4 * BLOCK) // 2
         up, down = slice(4 * BLOCK, 4 * BLOCK + ff), slice(4 * BLOCK + ff, 4 * BLOCK + 2 * ff)
@@ -695,6 +711,9 @@
         branch = ba[...] + branch_f
         xb[0] = x_two.astype(BF16)
         xb[1] = branch.astype(BF16)
+        if outputs_ready is not None:
+            outputs_ready()
+            tokens_ready()
         diff_x = x_two - tdo[0].astype(F32)
         diff_y = branch + tdo[1].astype(F32)
         loss = jnp.sum(self.live * (diff_x * diff_x + diff_y * diff_y))
@@ -734,7 +753,9 @@
         for i, vector in enumerate((gain_grad_a, bias_grad_a, gain_grad_f, bias_grad_f)):
             sums = jnp.where(lane == i, vector, sums)
         sums = jnp.where(lane == 4, loss, sums)
-        sm[...] = sums.T[:8]
+        sums = sums.T[:8]
+        for s in range(sm.shape[0]):
+            sm[s] = sums[:, s * sm.shape[2] : (s + 1) * sm.shape[2]]
 
 
 def layer_kernel(
@@ -769,7 +790,7 @@
             jax.ShapeDtypeStruct(xp.shape, BF16),
             jax.ShapeDtypeStruct(xc.shape, BF16),
             jax.ShapeDtypeStruct(weights.shape, BF16),
-            jax.ShapeDtypeStruct((8, full), F32),
+            jax.ShapeDtypeStruct((1, 8, full), F32),
         ),
         in_specs=[pl.BlockSpec(memory_space=pltpu.SMEM)] + [vmem] * 6,
         out_specs=[vmem] * 5,
@@ -800,6 +821,619 @@
     )(lengths, lengths, xp, xc, tdo, weights, vec)
 
 
+class Line:
+    def __init__(self, c):
+        self.c = c
+        self.mid = c * (3 - c) // 2 == 1
+        self.end = c * (3 - c) // 2 == 0
+        inner = c * (3 - c) // 2
+        far = 3 * (1 - c // 2)
+        one = c - 1 + 2 * ((4 - c) // 4)
+        self.near = [c, one, 6 - c - one - far, far]
+        self.pass_to = [None, c + 1, c - 1, 3 * (c - 1)]
+        last = 1 + c % 2
+        second = 6 - c - far - last
+        self.far = [far, second, last, c]
+        self.sum_to = [last, last + inner * (second - last), last]
+        self.slot = [far, second + 4 * inner * (2 - c), last + c // 2 * (4 - last)]
+
+
+class Traffic:
+    def __init__(self, at):
+        self.at = at
+        self.pending = {}
+
+    def start(self, key, make, cond=None):
+        if cond is None:
+            make().start()
+        else:
+            pl.when(cond)(lambda: make().start())
+        self.pending[key] = (make, cond)
+
+    def send(self, key, src, dst, send_sem, recv_sem, device, cond=None):
+        self.start(key, lambda: remote(src(), dst(), send_sem(), recv_sem(), device), cond)
+
+    def landed(self, dst, recv_sem):
+        remote(dst, dst, recv_sem, recv_sem, self.at.sibling).wait_recv()
+
+    def drain(self):
+        for make, cond in self.pending.values():
+            if cond is None:
+                make().wait_send()
+            else:
+                pl.when(cond)(lambda make=make: make().wait_send())
+
+
+def at_index(ref, *index):
+    return ref.at[index]
+
+
+class WeightGather:
+    def __init__(self, tag, traffic, line, w, cols, feat, sems):
+        self.tag, self.t, self.at, self.line = tag, traffic, traffic.at, line
+        self.w, self.cols, self.feat = w, cols, feat
+        self.col_s, self.col_r, self.one_s, self.one_r, self.two_s, self.two_r, self.sib_s, self.sib_r = sems
+
+    def piece(self, row, c, core):
+        half = self.feat // 2
+        rows = pl.ds(pl.multiple_of(c * self.feat + core * half, half), half)
+        return self.w.at[row, rows, self.cols]
+
+    def move(self, key, row, c, send_sem, recv_sem, device, cond=None):
+        here = functools.partial(self.piece, row, c, self.at.dp)
+        self.t.send(
+            (self.tag,) + key, here, here,
+            lambda: at_index(*send_sem), lambda: at_index(*recv_sem), device, cond,
+        )
+
+    def own(self):
+        at, line = self.at, self.line
+        c = line.c
+        for i in range(2):
+            self.move(
+                ("own", i), at.row, c, (self.col_s, i), (self.col_r, c),
+                at.col_dev(line.near[1 + i]), line.mid if i else None,
+            )
+        self.rows(0)
+
+    def rows(self, j):
+        at, c = self.at, self.line.near[j]
+        self.move(("one", j), at.row, c, (self.one_s, j), (self.one_r, j), at.first_dev)
+        self.move(("two", j), at.row, c, (self.two_s, 0, j), (self.two_r, 0, j), at.second_dev)
+        if j:
+            self.move(("sib", j), at.row, c, (self.sib_s, 0, j), (self.sib_r, 0, j), at.sibling)
+
+    def arrive(self, j):
+        at, c = self.at, self.line.near[j]
+        self.t.landed(self.piece(at.row, c, at.dp), self.col_r.at[c])
+        self.move(
+            ("pass", j), at.row, c, (self.col_s, 1 + j), (self.col_r, c),
+            at.col_dev(self.line.pass_to[j]), self.line.mid,
+        )
+        self.rows(j)
+
+    def first(self, j):
+        at, c = self.at, self.line.near[j]
+        self.t.landed(self.piece(at.first, c, at.dp), self.one_r.at[j])
+        self.move(("far", j), at.first, c, (self.two_s, 1, j), (self.two_r, 1, j), at.second_dev)
+        self.move(("sib1", j), at.first, c, (self.sib_s, 1, j), (self.sib_r, 1, j), at.sibling)
+
+    def second(self, j):
+        at, c = self.at, self.line.near[j]
+        for i, row in ((0, at.second), (1, at.both)):
+            self.t.landed(self.piece(row, c, at.dp), self.two_r.at[i, j])
+            self.move(
+                ("sib2", i, j), row, c, (self.sib_s, 2 + i, j), (self.sib_r, 2 + i, j), at.sibling
+            )
+
+    def finish(self):
+        at = self.at
+        for j in range(4):
+            c, core = self.line.near[j], 1 - at.dp
+            if j:
+                self.t.landed(self.piece(at.row, c, core), self.sib_r.at[0, j])
+            self.t.landed(self.piece(at.second, c, core), self.sib_r.at[1, j])
+            self.t.landed(self.piece(at.first, c, core), self.sib_r.at[2, j])
+            self.t.landed(self.piece(at.both, c, core), self.sib_r.at[3, j])
+
+
+class WeightScatter:
+    def __init__(self, tag, traffic, line, gw, cols, feat, sib, two, one, zb, out, sems):
+        self.tag, self.t, self.at, self.line = tag, traffic, traffic.at, line
+        self.gw, self.cols, self.feat = gw, cols, feat
+        self.sib, self.two, self.one, self.zb, self.out = sib, two, one, zb, out
+        self.sib_s, self.sib_r, self.two_s, self.two_r, self.one_s, self.one_r = sems[:6]
+        self.col_s, self.col_r, self.fin_s, self.fin_r = sems[6:]
+
+    def rows(self, i, core):
+        half = self.feat // 2
+        return pl.ds(pl.multiple_of(self.line.far[i] * self.feat + core * half, half), half)
+
+    def begin(self, i):
+        self.t.send(
+            (self.tag, "sib", i),
+            lambda: self.gw.at[:, self.rows(i, 1 - self.at.dp), self.cols],
+            lambda: self.sib.at[i],
+            lambda: self.sib_s.at[i], lambda: self.sib_r.at[i], self.at.sibling,
+        )
+
+    def step1(self, i):
+        at = self.at
+        self.t.landed(self.sib.at[i], self.sib_r.at[i])
+        for row in range(4):
+            here = self.gw[row, self.rows(i, at.dp), self.cols]
+            self.sib[i, row] = (here.astype(F32) + self.sib[i, row].astype(F32)).astype(BF16)
+        for n, row in ((1, at.both), (0, at.second)):
+            self.t.send(
+                (self.tag, "two", n, i),
+                lambda row=row: self.sib.at[i, row],
+                lambda n=n: self.two.at[n, i],
+                lambda n=n: self.two_s.at[n, i], lambda n=n: self.two_r.at[n, i], at.second_dev,
+            )
+
+    def step2(self, i):
+        at = self.at
+        self.t.landed(self.two.at[1, i], self.two_r.at[1, i])
+        total = self.sib[i, at.first].astype(F32) + self.two[1, i].astype(F32)
+        self.two[1, i] = total.astype(BF16)
+        self.t.send(
+            (self.tag, "one", i),
+            lambda: self.two.at[1, i], lambda: self.one.at[i],
+            lambda: self.one_s.at[i], lambda: self.one_r.at[i], at.first_dev,
+        )
+
+    def total(self, i):
+        near = self.sib[i, self.at.row].astype(F32) + self.two[0, i].astype(F32)
+        return near + self.one[i].astype(F32)
+
+    def step3(self, i):
+        line = self.line
+        self.t.landed(self.two.at[0, i], self.two_r.at[0, i])
+        self.t.landed(self.one.at[i], self.one_r.at[i])
+        if i < 3:
+
+            @pl.when(line.mid)
+            def _():
+                self.t.landed(self.zb.at[line.far[i]], self.col_r.at[line.far[i]])
+                total = self.total(i) + self.zb[line.far[i]].astype(F32)
+                self.two[0, i] = total.astype(BF16)
+
+            @pl.when(line.end)
+            def _():
+                self.two[0, i] = self.total(i).astype(BF16)
+
+            self.t.send(
+                (self.tag, "col", i),
+                lambda: self.two.at[0, i], lambda: self.zb.at[line.slot[i]],
+                lambda: self.col_s.at[i], lambda: self.col_r.at[line.slot[i]],
+                self.at.col_dev(line.sum_to[i]),
+            )
+            return
+        half = self.feat // 2
+        mine = pl.ds(pl.multiple_of(self.at.dp * half, half), half)
+        self.out[mine] = self.total(i)
+        for slot, cond in ((line.c, line.c > 0), (4, line.c < 3)):
+
+            @pl.when(cond)
+            def _(slot=slot):
+                self.t.landed(self.zb.at[slot], self.col_r.at[slot])
+                self.out[mine] += self.zb[slot].astype(F32)
+
+        self.t.send(
+            (self.tag, "fin"),
+            lambda: self.out.at[mine], lambda: self.out.at[mine],
+            lambda: self.fin_s, lambda: self.fin_r, self.at.sibling,
+        )
+
+    def finish(self):
+        half = self.feat // 2
+        other = pl.ds(pl.multiple_of((1 - self.at.dp) * half, half), half)
+        self.t.landed(self.out.at[other], self.fin_r)
+
+
+def step_kernel(
+    parts, lens_ref, len_table, x_ref, y_ref, tx_ref, ty_ref, wq_ref, wo_ref, wu_ref, wd_ref, vec_ref,
+    xout_ref, yout_ref, gx_ref, gy_ref, gq_ref, go_ref, gu_ref, gd_ref, gv_ref,
+    w, gw, xp, xc, xo, xt, kv, kvt, qt, att, lse, delta, d_att, s_scr, pf_scr, p_scr, ds_scr,
+    dsa, hid, acc, ba, dx, dxo, tdp, tdo, xb, xbo, vrow, gpb, gxz, gcb, gco, sm, smb, smz,
+    sib1, two1, one1, zb1, out1, sib2, two2, one2, zb2, out2,
+    xs, xr, cs, cr, ts, tr, vs, vr, bs, br, gs, gr, ks, kr, ss, sr, zs, zr, *wsems,
+):
+    ncol = 4
+    at = Places(ncol)
+    t = Traffic(at)
+    c = at.col
+    line = Line(c)
+    feat = x_ref.shape[0]
+    own = xo.shape[1]
+    cont = xc.shape[1]
+    qkv, rest = slice(0, 3 * BLOCK), slice(3 * BLOCK, w.shape[2])
+
+    def rows_of(s):
+        return pl.ds(pl.multiple_of(s * feat, feat), feat)
+
+    def own_cols(s):
+        return pl.ds(pl.multiple_of(s * own, own), own)
+
+    def cont_cols(s, first=0):
+        return pl.ds(pl.multiple_of(first + s * cont, cont), cont)
+
+    mine = rows_of(c)
+    at.meet()
+    gather1 = WeightGather("w1", t, line, w, qkv, feat, wsems[0:8])
+    gather2 = WeightGather("w2", t, line, w, rest, feat, wsems[8:16])
+
+    w[at.row, mine, qkv] = wq_ref[...]
+    gather1.own()
+    for i in range(2):
+        t.send(
+            ("x", i),
+            lambda: x_ref.at[:, :PROMPT], lambda: xp.at[mine],
+            lambda i=i: xs.at[i], lambda: xr.at[c],
+            at.col_dev(line.near[1 + i]), line.mid if i else None,
+        )
+    for k in range(1, ncol):
+        to = at.ahead(k)
+        t.send(
+            ("xc", k),
+            lambda to=to: x_ref.at[:, cont_cols(to, PROMPT)], lambda: xc.at[mine],
+            lambda k=k: cs.at[k], lambda k=k: cr.at[k], at.col_dev(to),
+        )
+    local = [
+        lambda: pltpu.make_async_copy(x_ref.at[:, :PROMPT], xp.at[mine], cs.at[0]),
+        lambda: pltpu.make_async_copy(x_ref.at[:, cont_cols(c, PROMPT)], xc.at[mine], cr.at[0]),
+    ]
+    for make in local:
+        make().start()
+    vrow[c] = vec_ref[...]
+    for k in range(1, ncol):
+        to = at.ahead(k)
+        t.send(
+            ("v", k),
+            lambda: vrow.at[c], lambda: vrow.at[c],
+            lambda k=k: vs.at[k], lambda k=k: vr.at[k], at.col_dev(to),
+        )
+    w[at.row, mine, 3 * BLOCK : 4 * BLOCK] = wo_ref[...].T
+    ff = wu_ref.shape[1]
+    w[at.row, mine, 4 * BLOCK : 4 * BLOCK + ff] = wu_ref[...]
+    w[at.row, mine, 4 * BLOCK + ff :] = wd_ref[...].T
+    gather2.own()
+
+    pieces = []
+    for p in range(parts):
+        pieces.append((p * own, p * BLOCK, BLOCK))
+        pieces.append((p * own + BLOCK, (2 * parts - 1 - p) * BLOCK, BLOCK))
+        pieces.append((p * own + PAIR, PROMPT + p * cont, cont))
+    for to, frm, width in pieces:
+        tdp[0, :, to : to + width] = tx_ref[:, frm : frm + width]
+        y_here = y_ref[:, frm : frm + width].astype(F32)
+        tdp[1, :, to : to + width] = (y_here - ty_ref[:, frm : frm + width].astype(F32)).astype(BF16)
+
+    def x_arrive(j):
+        s = line.near[j]
+        t.landed(xp.at[rows_of(s)], xr.at[s])
+        t.send(
+            ("xpass", j),
+            lambda: xp.at[rows_of(s)], lambda: xp.at[rows_of(s)],
+            lambda: xs.at[1 + j], lambda: xr.at[s],
+            at.col_dev(line.pass_to[j]), line.mid,
+        )
+
+    gather1.arrive(1)
+    gather1.arrive(2)
+    gather1.first(0)
+    gather1.arrive(3)
+    x_arrive(1)
+    x_arrive(2)
+    for j in range(1, 4):
+        gather1.first(j)
+    for j in range(4):
+        gather1.second(j)
+    gather2.arrive(1)
+    gather2.arrive(2)
+    gather2.first(0)
+    x_arrive(3)
+    for k in range(1, ncol):
+        t.landed(xc.at[rows_of(at.behind(k))], cr.at[k])
+    for make in local:
+        make().wait()
+    gather1.finish()
+
+    group = at.dp * lax.axis_size("row") + at.row
+    lens = [lens_ref[group, 0]] + [lens_ref[group, 1 + 2 * c + n] for n in range(2)]
+    count = jnp.sum(len_table[...].astype(F32))
+    total_tokens = lens_ref.shape[0] * GROUP
+    layer = Layer(c, parts, lens, total_tokens, count)
+    layer.project(xp, xc, w, xo, xt, kv, kvt, qt)
+
+    gather2.arrive(3)
+    for k in range(1, ncol):
+        to = at.ahead(k)
+        t.send(
+            ("td", k),
+            lambda to=to: tdp.at[:, :, own_cols(to)], lambda: tdo.at[:, mine],
+            lambda k=k: ts.at[k], lambda k=k: tr.at[k], at.col_dev(to),
+        )
+    tdo[:, mine] = tdp[:, :, own_cols(c)]
+
+    def forward_steps(r):
+        @pl.when(r == 0)
+        def _():
+            gather2.first(1)
+            gather2.first(2)
+
+        @pl.when(r == 1)
+        def _():
+            gather2.second(0)
+            gather2.second(1)
+
+        @pl.when(r == 2)
+        def _():
+            gather2.first(3)
+            gather2.second(2)
+
+        @pl.when(r == 3)
+        def _():
+            gather2.second(3)
+
+    layer.attend(kv, kvt, qt, att, lse, s_scr, pf_scr, forward_steps)
+    for k in range(1, ncol):
+        t.landed(vrow.at[at.behind(k)], vr.at[k])
+    gather2.finish()
+    vec = jnp.concatenate([vrow[s].T for s in range(ncol)], axis=0)
+
+    def tokens_ready():
+        for k in range(1, ncol):
+            t.landed(tdo.at[:, rows_of(at.behind(k))], tr.at[k])
+
+    def outputs_ready():
+        for k in range(1, ncol):
+            to = at.ahead(k)
+            t.send(
+                ("xb", k),
+                lambda to=to: xb.at[:, rows_of(to)], lambda: xbo.at[:, :, own_cols(c)],
+                lambda k=k: bs.at[k], lambda k=k: br.at[k], at.col_dev(to),
+            )
+        xbo[:, :, own_cols(c)] = xb[:, mine]
+
+    layer.middle(
+        xo, tdo, w, vec, att, xb, gw, sm, d_att, delta, dsa, hid, acc, ba, tokens_ready, outputs_ready
+    )
+
+    scatter1 = WeightScatter(
+        "g1", t, line, gw, qkv, feat, sib1, two1, one1, zb1, out1, wsems[16:26]
+    )
+    scatter2 = WeightScatter(
+        "g2", t, line, gw, rest, feat, sib2, two2, one2, zb2, out2, wsems[26:36]
+    )
+    for i in range(4):
+        scatter2.begin(i)
+
+    def small_send(i, src, device):
+        t.send(
+            ("sm", i), src, lambda: smb.at[i], lambda: ss.at[i], lambda: sr.at[i], device
+        )
+
+    small_send(0, lambda: sm, at.sibling)
+
+    def back_steps(r):
+        @pl.when(r == 0)
+        def _():
+            scatter2.step1(0)
+            scatter2.step1(1)
+            t.landed(smb.at[0], sr.at[0])
+            smb[3] = sm[...] + smb[0]
+            small_send(1, lambda: smb.at[3], at.second_dev)
+
+        @pl.when(r == 1)
+        def _():
+            scatter2.step1(2)
+            scatter2.step1(3)
+            t.landed(smb.at[1], sr.at[1])
+            smb[4] = smb[3] + smb[1]
+            small_send(2, lambda: smb.at[4], at.first_dev)
+
+        @pl.when(r == 2)
+        def _():
+            scatter2.step2(0)
+            t.landed(smb.at[2], sr.at[2])
+            smb[5] = smb[4] + smb[2]
+            for k in range(1, ncol):
+                to = at.ahead(k)
+                t.send(
+                    ("smz", k),
+                    lambda to=to: smb.at[5, to], lambda k=k: smz.at[k],
+                    lambda k=k: zs.at[k], lambda k=k: zr.at[k], at.col_dev(to),
+                )
+
+        @pl.when(r == 3)
+        def _():
+            scatter2.step2(1)
+
+    layer.attend_back(
+        kv, kvt, qt, lse, delta, d_att, kvt, qt, p_scr, ds_scr, back_steps, (xp, xc, xo, gw)
+    )
+    for i in range(4):
+        scatter1.begin(i)
+
+    def grad_block(s):
+        rows = rows_of(s)
+        for r in range(w.shape[0]):
+            part = dot_nn(w[r, rows, BLOCK : 3 * BLOCK], kvt[r])
+            mine_part = dot_nn(w[r, rows, :BLOCK], qt[r * BLOCK : (r + 1) * BLOCK])
+            if r == 0:
+                dx[...] = part
+                dxo[...] = dsa[rows] + mine_part
+            else:
+                dx[...] += part
+                dxo[...] += mine_part
+        low, high = layer.own_columns()
+        dx[:, low] += dxo[:, :BLOCK]
+        dx[:, high] += dxo[:, BLOCK:PAIR]
+        dx[:, PROMPT:] += dxo[:, PAIR:]
+
+    def grad_send(i):
+        s = line.far[i]
+        grad_block(s)
+
+        @pl.when(line.mid)
+        def _():
+            t.landed(gxz.at[s], gr.at[s])
+            gpb[i] = (dx[:, :PROMPT] + gxz[s].astype(F32)).astype(BF16)
+
+        @pl.when(line.end)
+        def _():
+            gpb[i] = dx[:, :PROMPT].astype(BF16)
+
+        t.send(
+            ("gx", i),
+            lambda: gpb.at[i], lambda: gxz.at[line.slot[i]],
+            lambda: gs.at[i], lambda: gr.at[line.slot[i]], at.col_dev(line.sum_to[i]),
+        )
+        gcb[i] = dx[:, PROMPT:].astype(BF16)
+        t.send(
+            ("gc", i),
+            lambda: gcb.at[i], lambda: gco.at[c],
+            lambda: ks.at[i], lambda: kr.at[c], at.col_dev(s),
+        )
+
+    grad_send(0)
+    scatter2.step2(2)
+    for i in range(4):
+        scatter1.step1(i)
+    grad_send(1)
+    scatter2.step2(3)
+    for i in range(4):
+        scatter1.step2(i)
+    grad_send(2)
+    scatter2.step3(0)
+    scatter2.step3(1)
+    grad_block(c)
+    gx_ref[:, :PROMPT] = dx[:, :PROMPT]
+    gx_ref[:, cont_cols(c, PROMPT)] = dx[:, PROMPT:]
+    scatter1.step3(0)
+    scatter1.step3(1)
+    scatter2.step3(2)
+    scatter1.step3(2)
+
+    for k in range(1, ncol):
+        t.landed(xbo.at[:, :, own_cols(at.behind(k))], br.at[k])
+    slot = iota((1, CONT), 1)
+    weight = jnp.concatenate(
+        [(iota((1, PROMPT), 1) < lens[0]).astype(F32)]
+        + [(slot < lens_ref[group, 1 + n]).astype(F32) for n in range(NCONT)],
+        axis=1,
+    ) * (total_tokens / count)
+    for frm, to, width in pieces:
+        cols = slice(to, to + width)
+        xout_ref[:, cols] = xbo[0, :, frm : frm + width]
+        branch = xbo[1, :, frm : frm + width].astype(F32)
+        y_here = y_ref[:, cols].astype(F32)
+        yout_ref[:, cols] = (y_here + branch).astype(BF16)
+        gy_ref[:, cols] = (y_here - ty_ref[:, cols].astype(F32) + branch) * weight[:, cols]
+
+    scatter2.step3(3)
+    scatter1.step3(3)
+    small = smb[5, c]
+    for k in range(1, ncol):
+        t.landed(smz.at[k], zr.at[k])
+        small = small + smz[k]
+    gv_ref[...] = small
+    for k in range(1, ncol):
+        s = at.behind(k)
+        t.landed(gco.at[s], kr.at[s])
+        gx_ref[:, cont_cols(s, PROMPT)] = gco[s].astype(F32)
+    for slot_at, cond in ((c, c > 0), (4, c < 3)):
+
+        @pl.when(cond)
+        def _(slot_at=slot_at):
+            t.landed(gxz.at[slot_at], gr.at[slot_at])
+            gx_ref[:, :PROMPT] += gxz[slot_at].astype(F32)
+
+    scatter2.finish()
+    scatter1.finish()
+    for i in range(3):
+        gq_ref[i] = out1[:, i * BLOCK : (i + 1) * BLOCK]
+    go_ref[...] = out2[:, :BLOCK].T
+    gu_ref[...] = out2[:, BLOCK : BLOCK + ff]
+    gd_ref[...] = out2[:, BLOCK + ff :].T
+    t.drain()
+
+
+def run_step(lengths, x, y, tx, ty, wq, wo, wu, wd, vec):
+    feat, tokens = x.shape
+    full = 4 * feat
+    ff = wu.shape[1]
+    width = 4 * BLOCK + 2 * ff
+    rest = BLOCK + 2 * ff
+    half = feat // 2
+    own, cont = tokens // 4, NCONT * CONT // 4
+    keys = PROMPT + cont
+    heads = full // HD
+    vmem = pl.BlockSpec(memory_space=pltpu.VMEM)
+    dma = pltpu.SemaphoreType.DMA
+
+    def bf(*shape):
+        return pltpu.VMEM(shape, BF16)
+
+    def f32(*shape):
+        return pltpu.VMEM(shape, F32)
+
+    def reduce_buffers(cols):
+        return [
+            bf(4, 4, half, cols), bf(2, 4, half, cols), bf(4, half, cols), bf(5, half, cols), f32(feat, cols),
+        ]
+
+    gather_sems = [
+        dma((5,)), dma((4,)), dma((4,)), dma((4,)), dma((2, 4)), dma((2, 4)), dma((4, 4)), dma((4, 4)),
+    ]
+    scatter_sems = [
+        dma((4,)), dma((4,)), dma((2, 4)), dma((2, 4)), dma((4,)), dma((4,)), dma((3,)), dma((5,)),
+        dma(()), dma(()),
+    ]
+    sums = (4, 8, feat)
+    return pl.pallas_call(
+        functools.partial(step_kernel, 4),
+        out_shape=(
+            jax.ShapeDtypeStruct((feat, tokens), BF16),
+            jax.ShapeDtypeStruct((feat, tokens), BF16),
+            jax.ShapeDtypeStruct((feat, tokens), F32),
+            jax.ShapeDtypeStruct((feat, tokens), F32),
+            jax.ShapeDtypeStruct((3, feat, BLOCK), F32),
+            jax.ShapeDtypeStruct(wo.shape, F32),
+            jax.ShapeDtypeStruct(wu.shape, F32),
+            jax.ShapeDtypeStruct(wd.shape, F32),
+            jax.ShapeDtypeStruct((8, feat), F32),
+        ),
+        in_specs=[pl.BlockSpec(memory_space=pltpu.SMEM), vmem, pl.BlockSpec(memory_space=pl.ANY)]
+        + [vmem] * 8,
+        out_specs=[vmem] * 9,
+        scratch_shapes=[
+            bf(4, full, width), bf(4, full, width), bf(full, PROMPT), bf(full, cont), bf(full, own),
+            bf(keys, full), bf(keys, 4 * PAIR), bf(4, PAIR, keys), bf(full, own), bf(full, own),
+            f32(heads, own), f32(heads, own), bf(full, own), f32(2, PROMPT, PAIR), bf(2, PROMPT, PAIR),
+            bf(2, PROMPT, own), bf(2, PROMPT, own), f32(full, own), bf(4, own, ff), f32(full, own),
+            f32(full, own), f32(feat, keys), f32(feat, own), bf(2, feat, tokens), bf(2, full, own),
+            bf(2, full, own), bf(2, feat, tokens), f32(4, 8, feat), bf(3, feat, PROMPT),
+            bf(5, feat, PROMPT), bf(3, feat, cont), bf(4, feat, cont),
+            f32(*sums), f32(6, *sums), f32(*sums),
+        ]
+        + reduce_buffers(3 * BLOCK)
+        + reduce_buffers(rest)
+        + [
+            dma((5,)), dma((4,)), dma((4,)), dma((4,)), dma((4,)), dma((4,)), dma((4,)), dma((4,)),
+            dma((4,)), dma((4,)), dma((3,)), dma((5,)), dma((3,)), dma((4,)), dma((3,)), dma((3,)),
+            dma((4,)), dma((4,)),
+        ]
+        + gather_sems * 2
+        + scatter_sems * 2,
+        compiler_params=pltpu.CompilerParams(
+            collective_id=2, has_side_effects=True, vmem_limit_bytes=61 << 20
+        ),
+        name="layer_step",
+    )(lengths, lengths, x, y, tx, ty, wq, wo, wu, wd, vec)
+
+
 def body(
     x_stream, y_stream, w_qkv, w_out, gain_attn, bias_attn, w_up, w_down, gain_ffn, bias_ffn,
     teach_x, teach_y, lengths,
@@ -813,6 +1447,18 @@
     block = w_qkv.shape[2]
     ff_block = w_up.shape[1]
 
+    if ncol == parts:
+        small_vecs = jnp.stack([gain_attn, bias_attn, gain_ffn, bias_ffn] * 2).astype(F32)
+        x_out, y_out, grad_x, grad_y, g_q, g_o, g_u, g_d, sums = run_step(
+            lengths, x_stream, y_stream, teach_x, teach_y, w_qkv.reshape(feat, 3 * block),
+            w_out, w_up, w_down, small_vecs,
+        )
+        loss = sums[4, 0] / (2.0 * jnp.sum(lengths).astype(F32) * full)
+        return (
+            x_out, y_out, grad_x, grad_y, g_q.transpose(1, 0, 2), g_o, sums[0], sums[1], g_u, g_d,
+            sums[2], sums[3], loss,
+        )
+
     y_f32 = y_stream.astype(F32)
     dy = y_f32 - teach_y.astype(F32)
     teach_dy = to_parts(jnp.stack([teach_x, dy.astype(BF16)]), parts)
@@ -828,7 +1474,7 @@
     vec = jnp.pad(vecs.T, ((0, 0), (0, 124)))
     xb, gp, gc, gw, small = run_layer(lengths, x_prompt, x_cont, tdo, weights, vec, parts)
     lanes = max(feat, 128)
-    small = small.reshape(8, ncol, feat).transpose(1, 0, 2)
+    small = small[0].reshape(8, ncol, feat).transpose(1, 0, 2)
     small = jnp.pad(small, ((0, 0), (0, 0), (0, lanes - feat)))
     xb, gp, gc, gw, sums = scatter_all(xb, gp, gc, gw, small, ncol, parts)
 

time: 240 us -> 169 us (0.70)
  Pallas kernels: 202 us -> 148 us
  blocking collectives: 10.5 us -> 0 us
  other arithmetic: 9.96 us -> 1.92 us
    pallas_call x3 -> x1, Pallas kernels: 202 us -> 148 us  [run_step(): pl.pallas_call(functools.partial(step_kernel, 4), out_shape=(jax.ShapeDty...]
    all_gather x1 -> x0, blocking collectives: 10.5 us -> none  [body(): vecs = lax.all_gather(small_vecs, 'col', axis=1, tiled=True)]
    unnamed x37 -> x33, local copies, waits for them, and re-layouts: 3.03 us -> 11.1 us
    reshape x7 -> x0, local copies, waits for them, and re-layouts: 3.91 us -> none  [the longest x1 1.59 us: to_parts(): return jnp.concatenate([prompt, cont], axis=-1).reshape(array_in.shape)]
    reshape x4 -> x0, other arithmetic: 3.45 us -> none  [the longest x1 1.14 us: to_parts(): split = array_in.reshape(lead + (groups, GROUP))]
where the time goes in v1:
time: 169 us; the launch traced here: 167 us
  Pallas kernels  148 us (88%)
  local copies, waits for them, and re-layouts  13.6 us (8%)
  between operations  3.16 us (2%)
  other arithmetic  1.92 us (1%)
    pallas_call x1, Pallas kernels, run_step(): pl.pallas_call(functools.partial(step_kernel, 4), out_shape=(jax.ShapeDty...  148 us
    unnamed x33, local copies, waits for them, and re-layouts  11.1 us

profile of v1, /device:TPU:13, one launch (start us, length us, event | category | flops | bytes accessed | tf_op | source)
XLA Modules:
  0.0 166.9 jit_solution(12533187206530481046)
XLA Ops:
  0.6 1.3 reduce_sum.9
  2.7 0.6 copy-done.10
  3.3 0.0 copy-done.7
  3.3 0.0 copy-done.8
  3.3 0.0 copy-done.9
  3.4 0.6 convert_element_type.6.vec_ref
  4.0 1.0 copy.27
  5.0 0.8 copy.28.wq_ref
  5.7 148.2 %layer_step.1 = (bf16[128,2048]{1,0:T(8,128)(2,1)}, bf16[128,2048]{1,0:T(8,128)(2,1)}, f32[128,2048]{1,0:T(8,128)}, f32[128,2048]{1,0:T(8,128)}, f32[3,128,128]{...) custom-call(s32[8,9]{1,0:T(8,128)} %len_table.1, ...), custom_call_target="tpu_custom_call" | custom-call | tf_op jit(solution)/shard_map/layer_step/pallas_call | solution.py:1395
  153.9 1.2 slice.19
  155.8 0.7 copy-done.11
  156.5 0.5 slice_bitcast_fusion
  157.0 2.0 %copy.37 = bf16[128,2048]{1,0:T(8,128)(2,1)} copy(bf16[128,2048]{1,0:T(8,128)(2,1)} %get-tuple-element.48) | data formatting | bytes 1048576
  159.0 0.8 copy.38
  159.8 1.0 copy.39
  160.7 0.6 copy-done
  161.4 1.0 copy.40
  162.3 0.1 copy-done.5
  162.5 0.7 copy.41
  163.2 0.2 copy-done.6
  163.4 0.6 copy.42
  164.0 0.7 copy.43
  164.7 0.3 copy-done.3
  165.0 0.7 copy.44
  (16 shorter events, 0.1 us)
Async XLA Ops:
  2.6 0.7 copy-start.10
  2.6 0.7 copy-start.7
  2.6 0.7 copy-start.8
  2.7 0.7 copy-start.9
  155.8 0.7 copy-start.11
  156.5 2.5 %copy-start.2 = (bf16[128,2048]{1,0:T(8,128)(2,1)S(1)}, bf16[128,2048]{1,0:T(8,128)(2,1)}, u32[]{:S(2)}) copy-start(bf16[128,2048]{1,0:T(8,128)(2,1)} %get-tuple-element.49) | copy-start | bytes 1572868
  157.0 2.8 %copy-start.1 = (f32[128,2048]{1,0:T(8,128)S(1)}, f32[128,2048]{1,0:T(8,128)}, u32[]{:S(2)}) copy-start(f32[128,2048]{1,0:T(8,128)} %get-tuple-element.50) | copy-start | bytes 3145732
  159.8 1.6 copy-start
  161.4 1.1 copy-start.5
  162.5 0.9 copy-start.6
  162.5 1.5 copy-start.4
  164.0 1.0 copy-start.3

commit v2 on v1

--- a/solution.py
+++ b/solution.py
@@ -501,9 +501,16 @@
 PAIR = 2 * BLOCK
 
 
+def put(ref, r, cols, value):
+    lead = ref.shape[1:-1]
+    index = (r,) + (slice(None),) * len(lead) + (cols,)
+    ref[index] = value.astype(BF16).reshape(lead + (value.shape[1],))
+
+
 class Layer:
-    def __init__(self, part, parts, lens, total_tokens, count):
+    def __init__(self, part, parts, lens, total_tokens, count, order=lambda n: n):
         self.part, self.parts = part, parts
+        self.order = order
         self.lens = lens
         self.total_tokens, self.count = total_tokens, count
         slot = iota((1, BLOCK), 1)
@@ -610,7 +617,8 @@
     def attend_back(
         self, kv, kvt, qt, lse, delta, d_att, dkvt, dqt, p_scr, ds_scr, between=None, grads=None
     ):
-        def step(r, carry):
+        def step(n, carry):
+            r = self.order(n)
             k_cols = pl.ds(pl.multiple_of(r * PAIR, PAIR), BLOCK)
             v_cols = pl.ds(pl.multiple_of(r * PAIR + BLOCK, BLOCK), BLOCK)
             pair = pl.ds(pl.multiple_of(r * BLOCK, BLOCK), BLOCK)
@@ -635,10 +643,10 @@
                         ds_scr[head, keys, columns] = (prob * (dprob - dlt[:, columns])).astype(BF16)
                 d_query = dot_nn(kvt[r, k_rows, :PROMPT], ds_scr[head])
                 own_dq = [jnp.zeros((HD, PAIR), F32)]
-                for n in range(2):
-                    keys = slice(PROMPT + n * BLOCK, PROMPT + (n + 1) * BLOCK)
-                    lanes = slice(PAIR + n * BLOCK, PAIR + (n + 1) * BLOCK)
-                    score = self.masked_own(dot_nn(kv[keys, k_cols], query[:, lanes]), n)
+                for m in range(2):
+                    keys = slice(PROMPT + m * BLOCK, PROMPT + (m + 1) * BLOCK)
+                    lanes = slice(PAIR + m * BLOCK, PAIR + (m + 1) * BLOCK)
+                    score = self.masked_own(dot_nn(kv[keys, k_cols], query[:, lanes]), m)
                     prob = jnp.exp(score - norm[:, lanes])
                     dprob = dot_nn(kv[keys, v_cols], d_out[:, lanes])
                     d_score = (prob * (dprob - dlt[:, lanes])).astype(BF16)
@@ -653,16 +661,15 @@
             if grads is not None:
                 self.projection_grads(r, pair, *grads, dkvt, dqt)
             if between is not None:
-                between(r)
+                between(n)
             return carry
 
         lax.fori_loop(0, kvt.shape[0], step, 0)
 
     def projection_grads(self, r, rows, xp, xc, xo, gw, dkvt, dqt):
-        gw[r, :, :BLOCK] = dot_nt(xo[...], dqt[rows]).astype(BF16)
-        gw[r, :, BLOCK : 3 * BLOCK] = (
-            dot_nt(xp[...], dkvt[r, :, :PROMPT]) + dot_nt(xc[...], dkvt[r, :, PROMPT:])
-        ).astype(BF16)
+        put(gw, r, slice(0, BLOCK), dot_nt(xo[...], dqt[rows]))
+        both = dot_nt(xp[...], dkvt[r, :, :PROMPT]) + dot_nt(xc[...], dkvt[r, :, PROMPT:])
+        put(gw, r, slice(BLOCK, 3 * BLOCK), both)
 
     def input_grads(self, xp, xc, xo, w, dkvt, dqt, dsa, gp, gc, gw, dx, dxo):
         for r in range(w.shape[0]):
@@ -685,7 +692,7 @@
 
     def middle(
         self, xo, tdo, w, vec, att, xb, gw, sm, d_att, delta, dsa, hid, acc, ba,
-        tokens_ready=None, outputs_ready=None,
+        tokens_ready=None, outputs_ready=None, grads_ready=None, back_done=None,
     ):
         nrow, full = w.shape[0], w.shape[1]
         ff = (w.shape[2] - 4 * BLOCK) // 2
@@ -724,23 +731,28 @@
         d_branch_t = d_branch_f.T
         acc[...] = d_sum_f
 
-        def back(r, carry):
+        def back(n, carry):
+            r = self.order(n)
             hidden = hid[r]
             d_hidden = dot_nn(d_branch_t, w[r, :, down])
             d_pre = jnp.where(hidden.astype(F32) > 0, d_hidden, 0.0).astype(BF16)
-            gw[r, :, up] = dot_nn(x_low, d_pre).astype(BF16)
-            gw[r, :, down] = dot_nn(d_branch_f, hidden).astype(BF16)
+            put(gw, r, up, dot_nn(x_low, d_pre))
+            put(gw, r, down, dot_nn(d_branch_f, hidden))
             acc[...] += dot_nt(w[r, :, up], d_pre)
+            if grads_ready is not None:
+                grads_ready(n)
             return carry
 
         lax.fori_loop(0, nrow, back, 0)
+        if back_done is not None:
+            back_done()
         d_sum_a, gain_grad_a, bias_grad_a = norm_backward(acc[...], unit_a, inv_a, gain_a)
         dsa[...] = d_sum_a
         d_branch_a = (d_sum_a + grad_y).astype(BF16)
         for r in range(nrow):
             rows = slice(r * BLOCK, (r + 1) * BLOCK)
             attended = att[rows]
-            gw[r, :, 3 * BLOCK : 4 * BLOCK] = dot_nt(d_branch_a, attended).astype(BF16)
+            put(gw, r, slice(3 * BLOCK, 4 * BLOCK), dot_nt(d_branch_a, attended))
             d_here = dot_tn(w[r, :, 3 * BLOCK : 4 * BLOCK], d_branch_a).astype(BF16)
             d_att[rows] = d_here
             product = attended.astype(F32) * d_here.astype(F32)
@@ -937,88 +949,114 @@
             self.t.landed(self.piece(at.both, c, core), self.sib_r.at[3, j])
 
 
-class WeightScatter:
-    def __init__(self, tag, traffic, line, gw, cols, feat, sib, two, one, zb, out, sems):
-        self.tag, self.t, self.at, self.line = tag, traffic, traffic.at, line
-        self.gw, self.cols, self.feat = gw, cols, feat
-        self.sib, self.two, self.one, self.zb, self.out = sib, two, one, zb, out
-        self.sib_s, self.sib_r, self.two_s, self.two_r, self.one_s, self.one_r = sems[:6]
-        self.col_s, self.col_r, self.fin_s, self.fin_r = sems[6:]
-
-    def rows(self, i, core):
-        half = self.feat // 2
-        return pl.ds(pl.multiple_of(self.line.far[i] * self.feat + core * half, half), half)
-
-    def begin(self, i):
+def row_order(row, n):
+    return (row % 2 + (3 - n) // 2) % 2 + 2 * ((row // 2 + n + 1) % 2)
+
+
+class LineSum:
+    def __init__(self, tag, traffic, line, out, landing, sems):
+        self.tag, self.t, self.line = tag, traffic, line
+        self.out, self.landing = out, landing
+        self.send_s, self.recv_s = sems
+
+    def send(self, i, value):
+        line = self.line
+        s = line.far[i]
+
+        @pl.when(line.mid)
+        def _():
+            self.t.landed(self.landing.at[s], self.recv_s.at[s])
+            self.out[i] = (value() + self.landing[s].astype(F32)).astype(BF16)
+
+        @pl.when(line.end)
+        def _():
+            self.out[i] = value().astype(BF16)
+
         self.t.send(
-            (self.tag, "sib", i),
-            lambda: self.gw.at[:, self.rows(i, 1 - self.at.dp), self.cols],
-            lambda: self.sib.at[i],
-            lambda: self.sib_s.at[i], lambda: self.sib_r.at[i], self.at.sibling,
-        )
-
-    def step1(self, i):
-        at = self.at
-        self.t.landed(self.sib.at[i], self.sib_r.at[i])
-        for row in range(4):
-            here = self.gw[row, self.rows(i, at.dp), self.cols]
-            self.sib[i, row] = (here.astype(F32) + self.sib[i, row].astype(F32)).astype(BF16)
-        for n, row in ((1, at.both), (0, at.second)):
-            self.t.send(
-                (self.tag, "two", n, i),
-                lambda row=row: self.sib.at[i, row],
-                lambda n=n: self.two.at[n, i],
-                lambda n=n: self.two_s.at[n, i], lambda n=n: self.two_r.at[n, i], at.second_dev,
-            )
-
-    def step2(self, i):
-        at = self.at
-        self.t.landed(self.two.at[1, i], self.two_r.at[1, i])
-        total = self.sib[i, at.first].astype(F32) + self.two[1, i].astype(F32)
-        self.two[1, i] = total.astype(BF16)
-        self.t.send(
-            (self.tag, "one", i),
-            lambda: self.two.at[1, i], lambda: self.one.at[i],
-            lambda: self.one_s.at[i], lambda: self.one_r.at[i], at.first_dev,
-        )
-
-    def total(self, i):
-        near = self.sib[i, self.at.row].astype(F32) + self.two[0, i].astype(F32)
-        return near + self.one[i].astype(F32)
-
-    def step3(self, i):
-        line = self.line
-        self.t.landed(self.two.at[0, i], self.two_r.at[0, i])
-        self.t.landed(self.one.at[i], self.one_r.at[i])
-        if i < 3:
-
-            @pl.when(line.mid)
-            def _():
-                self.t.landed(self.zb.at[line.far[i]], self.col_r.at[line.far[i]])
-                total = self.total(i) + self.zb[line.far[i]].astype(F32)
-                self.two[0, i] = total.astype(BF16)
-
-            @pl.when(line.end)
-            def _():
-                self.two[0, i] = self.total(i).astype(BF16)
-
-            self.t.send(
-                (self.tag, "col", i),
-                lambda: self.two.at[0, i], lambda: self.zb.at[line.slot[i]],
-                lambda: self.col_s.at[i], lambda: self.col_r.at[line.slot[i]],
-                self.at.col_dev(line.sum_to[i]),
-            )
-            return
-        half = self.feat // 2
-        mine = pl.ds(pl.multiple_of(self.at.dp * half, half), half)
-        self.out[mine] = self.total(i)
-        for slot, cond in ((line.c, line.c > 0), (4, line.c < 3)):
+            (self.tag, "col", i),
+            lambda: self.out.at[i], lambda: self.landing.at[line.slot[i]],
+            lambda: self.send_s.at[i], lambda: self.recv_s.at[line.slot[i]],
+            self.t.at.col_dev(line.sum_to[i]),
+        )
+
+    def receive(self, add):
+        for slot, cond in ((self.line.c, self.line.c > 0), (4, self.line.c < 3)):
 
             @pl.when(cond)
             def _(slot=slot):
-                self.t.landed(self.zb.at[slot], self.col_r.at[slot])
-                self.out[mine] += self.zb[slot].astype(F32)
-
+                self.t.landed(self.landing.at[slot], self.recv_s.at[slot])
+                add(self.landing[slot].astype(F32))
+
+
+class WeightScatter:
+    def __init__(self, tag, traffic, line, gw, cols, sib, two, one, zs, zb, out, sems):
+        self.tag, self.t, self.at, self.line = tag, traffic, traffic.at, line
+        self.gw, self.cols = gw, cols
+        self.sib, self.two, self.one, self.out = sib, two, one, out
+        self.sib_s, self.sib_r, self.two_s, self.two_r, self.one_s, self.one_r = sems[:6]
+        self.fin_s, self.fin_r = sems[8:]
+        self.zs, self.zb, self.col_s, self.col_r = zs, zb, sems[6], sems[7]
+        self.half = out.shape[0] // 2
+
+    def begin(self, n):
+        self.t.send(
+            (self.tag, "sib", n),
+            lambda: self.gw.at[row_order(self.at.row, n), :, 1 - self.at.dp, :, self.cols],
+            lambda: self.sib.at[row_order(self.at.row, n)],
+            lambda: self.sib_s.at[n], lambda: self.sib_r.at[n], self.at.sibling,
+        )
+
+    def across(self, n, row):
+        self.t.send(
+            (self.tag, "two", n),
+            lambda: self.sib.at[row], lambda: self.two.at[n],
+            lambda: self.two_s.at[n], lambda: self.two_r.at[n], self.at.second_dev,
+        )
+
+    def merge(self, n):
+        r = row_order(self.at.row, n)
+        self.t.landed(self.sib.at[r], self.sib_r.at[n])
+        for c in range(4):
+            here = self.gw[r, c, self.at.dp, :, self.cols]
+            self.sib[r, c] = here + self.sib[r, c]
+        if n == 0:
+            self.across(1, self.at.both)
+        if n == 2:
+            self.across(0, self.at.second)
+
+    def step2(self):
+        self.t.landed(self.two.at[1], self.two_r.at[1])
+        for c in range(4):
+            self.two[1, c] = self.sib[self.at.first, c] + self.two[1, c]
+        self.t.send(
+            (self.tag, "one"),
+            lambda: self.two.at[1], lambda: self.one,
+            lambda: self.one_s, lambda: self.one_r, self.at.first_dev,
+        )
+
+    def total(self, c):
+        near = self.sib[self.at.row, c].astype(F32) + self.two[0, c].astype(F32)
+        return near + self.one[c].astype(F32)
+
+    def step3(self):
+        self.t.landed(self.two.at[0], self.two_r.at[0])
+        self.t.landed(self.one, self.one_r)
+        for k in range(1, 4):
+            to = self.at.ahead(k)
+            self.zs[k - 1] = self.total(to).astype(BF16)
+            self.t.send(
+                (self.tag, "col", k),
+                lambda k=k: self.zs.at[k - 1], lambda k=k: self.zb.at[k - 1],
+                lambda k=k: self.col_s.at[k - 1], lambda k=k: self.col_r.at[k - 1], self.at.col_dev(to),
+            )
+
+    def step4(self):
+        mine = pl.ds(pl.multiple_of(self.at.dp * self.half, self.half), self.half)
+        total = self.total(self.line.c)
+        for k in range(3):
+            self.t.landed(self.zb.at[k], self.col_r.at[k])
+            total = total + self.zb[k].astype(F32)
+        self.out[mine] = total
         self.t.send(
             (self.tag, "fin"),
             lambda: self.out.at[mine], lambda: self.out.at[mine],
@@ -1026,18 +1064,18 @@
         )
 
     def finish(self):
-        half = self.feat // 2
-        other = pl.ds(pl.multiple_of((1 - self.at.dp) * half, half), half)
+        other = pl.ds(pl.multiple_of((1 - self.at.dp) * self.half, self.half), self.half)
         self.t.landed(self.out.at[other], self.fin_r)
 
 
 def step_kernel(
-    parts, lens_ref, len_table, x_ref, y_ref, tx_ref, ty_ref, wq_ref, wo_ref, wu_ref, wd_ref, vec_ref,
-    xout_ref, yout_ref, gx_ref, gy_ref, gq_ref, go_ref, gu_ref, gd_ref, gv_ref,
-    w, gw, xp, xc, xo, xt, kv, kvt, qt, att, lse, delta, d_att, s_scr, pf_scr, p_scr, ds_scr,
-    dsa, hid, acc, ba, dx, dxo, tdp, tdo, xb, xbo, vrow, gpb, gxz, gcb, gco, sm, smb, smz,
-    sib1, two1, one1, zb1, out1, sib2, two2, one2, zb2, out2,
-    xs, xr, cs, cr, ts, tr, vs, vr, bs, br, gs, gr, ks, kr, ss, sr, zs, zr, *wsems,
+    parts, lens_ref, len_table, x_ref, y_hbm, tx_hbm, ty_hbm, wq_ref, wo_ref, wu_ref, wd_ref,
+    va_ref, vb_ref, vc_ref, vd_ref,
+    xbo, gco, gx_ref, out1, out2, gv_ref,
+    y_ref, tx_ref, ty_ref, w, gw, xp, xc, xo, xt, kv, kvt, qt, att, lse, delta, d_att, s_scr, pf_scr, p_scr, ds_scr,
+    dsa, hid, acc, ba, dx, dxo, tdp, tdo, xb, vrow, gpb, gxz, gcb, sm, smb, smz,
+    sib1, two1, one1, zs1, zb1, sib2, two2, one2, zs2, zb2,
+    xs, xr, cs, cr, ts, tr, vs, vr, bs, br, gs, gr, ks, kr, ss, sr, zs, zr, ls, *wsems,
 ):
     ncol = 4
     at = Places(ncol)
@@ -1047,7 +1085,7 @@
     feat = x_ref.shape[0]
     own = xo.shape[1]
     cont = xc.shape[1]
-    qkv, rest = slice(0, 3 * BLOCK), slice(3 * BLOCK, w.shape[2])
+    near, rest = slice(0, 4 * BLOCK), slice(4 * BLOCK, w.shape[2])
 
     def rows_of(s):
         return pl.ds(pl.multiple_of(s * feat, feat), feat)
@@ -1059,12 +1097,24 @@
         return pl.ds(pl.multiple_of(first + s * cont, cont), cont)
 
     mine = rows_of(c)
+    staged = [
+        pltpu.make_async_copy(src, dst, ls.at[i])
+        for i, (src, dst) in enumerate(((y_hbm, y_ref), (tx_hbm, tx_ref), (ty_hbm, ty_ref)))
+    ]
+    for copy in staged:
+        copy.start()
     at.meet()
-    gather1 = WeightGather("w1", t, line, w, qkv, feat, wsems[0:8])
+    gather1 = WeightGather("w1", t, line, w, near, feat, wsems[0:8])
     gather2 = WeightGather("w2", t, line, w, rest, feat, wsems[8:16])
 
-    w[at.row, mine, qkv] = wq_ref[...]
+    for i in range(3):
+        w[at.row, mine, i * BLOCK : (i + 1) * BLOCK] = wq_ref[:, i, :]
+    w[at.row, mine, 3 * BLOCK : 4 * BLOCK] = wo_ref[...].T
     gather1.own()
+    ff = wu_ref.shape[1]
+    w[at.row, mine, 4 * BLOCK : 4 * BLOCK + ff] = wu_ref[...]
+    w[at.row, mine, 4 * BLOCK + ff :] = wd_ref[...].T
+    gather2.own()
     for i in range(2):
         t.send(
             ("x", i),
@@ -1085,7 +1135,8 @@
     ]
     for make in local:
         make().start()
-    vrow[c] = vec_ref[...]
+    rows = [ref[...].astype(F32).reshape(1, feat) for ref in (va_ref, vb_ref, vc_ref, vd_ref)]
+    vrow[c] = jnp.concatenate(rows + rows, axis=0)
     for k in range(1, ncol):
         to = at.ahead(k)
         t.send(
@@ -1093,17 +1144,9 @@
             lambda: vrow.at[c], lambda: vrow.at[c],
             lambda k=k: vs.at[k], lambda k=k: vr.at[k], at.col_dev(to),
         )
-    w[at.row, mine, 3 * BLOCK : 4 * BLOCK] = wo_ref[...].T
-    ff = wu_ref.shape[1]
-    w[at.row, mine, 4 * BLOCK : 4 * BLOCK + ff] = wu_ref[...]
-    w[at.row, mine, 4 * BLOCK + ff :] = wd_ref[...].T
-    gather2.own()
-
-    pieces = []
-    for p in range(parts):
-        pieces.append((p * own, p * BLOCK, BLOCK))
-        pieces.append((p * own + BLOCK, (2 * parts - 1 - p) * BLOCK, BLOCK))
-        pieces.append((p * own + PAIR, PROMPT + p * cont, cont))
+    pieces = order_pieces(parts)
+    for copy in staged:
+        copy.wait()
     for to, frm, width in pieces:
         tdp[0, :, to : to + width] = tx_ref[:, frm : frm + width]
         y_here = y_ref[:, frm : frm + width].astype(F32)
@@ -1121,18 +1164,23 @@
 
     gather1.arrive(1)
     gather1.arrive(2)
+    gather2.arrive(1)
+    gather2.arrive(2)
     gather1.first(0)
+    gather2.first(0)
     gather1.arrive(3)
+    gather2.arrive(3)
     x_arrive(1)
     x_arrive(2)
     for j in range(1, 4):
         gather1.first(j)
     for j in range(4):
         gather1.second(j)
-    gather2.arrive(1)
-    gather2.arrive(2)
-    gather2.first(0)
+    gather2.first(1)
+    gather2.first(2)
+    gather2.second(0)
     x_arrive(3)
+    gather2.first(3)
     for k in range(1, ncol):
         t.landed(xc.at[rows_of(at.behind(k))], cr.at[k])
     for make in local:
@@ -1143,10 +1191,9 @@
     lens = [lens_ref[group, 0]] + [lens_ref[group, 1 + 2 * c + n] for n in range(2)]
     count = jnp.sum(len_table[...].astype(F32))
     total_tokens = lens_ref.shape[0] * GROUP
-    layer = Layer(c, parts, lens, total_tokens, count)
+    layer = Layer(c, parts, lens, total_tokens, count, functools.partial(row_order, at.row))
     layer.project(xp, xc, w, xo, xt, kv, kvt, qt)
 
-    gather2.arrive(3)
     for k in range(1, ncol):
         to = at.ahead(k)
         t.send(
@@ -1159,20 +1206,13 @@
     def forward_steps(r):
         @pl.when(r == 0)
         def _():
-            gather2.first(1)
-            gather2.first(2)
+            gather2.second(1)
 
         @pl.when(r == 1)
         def _():
-            gather2.second(0)
-            gather2.second(1)
+            gather2.second(2)
 
         @pl.when(r == 2)
-        def _():
-            gather2.first(3)
-            gather2.second(2)
-
-        @pl.when(r == 3)
         def _():
             gather2.second(3)
 
@@ -1194,20 +1234,28 @@
                 lambda to=to: xb.at[:, rows_of(to)], lambda: xbo.at[:, :, own_cols(c)],
                 lambda k=k: bs.at[k], lambda k=k: br.at[k], at.col_dev(to),
             )
-        xbo[:, :, own_cols(c)] = xb[:, mine]
-
-    layer.middle(
-        xo, tdo, w, vec, att, xb, gw, sm, d_att, delta, dsa, hid, acc, ba, tokens_ready, outputs_ready
-    )
+        pltpu.make_async_copy(xb.at[:, mine], xbo.at[:, :, own_cols(c)], bs.at[0]).start()
 
     scatter1 = WeightScatter(
-        "g1", t, line, gw, qkv, feat, sib1, two1, one1, zb1, out1, wsems[16:26]
+        "g1", t, line, gw, near, sib1, two1, one1, zs1, zb1, out1, wsems[16:26]
     )
     scatter2 = WeightScatter(
-        "g2", t, line, gw, rest, feat, sib2, two2, one2, zb2, out2, wsems[26:36]
+        "g2", t, line, gw, rest, sib2, two2, one2, zs2, zb2, out2, wsems[26:36]
     )
-    for i in range(4):
-        scatter2.begin(i)
+    x_sum = LineSum("gx", t, line, gpb, gxz, (gs, gr))
+
+    def begin_after(scatter, n):
+        for i in range(4):
+            pl.when(n == i)(lambda i=i: scatter.begin(i))
+
+    def back_done():
+        scatter2.merge(0)
+        scatter2.merge(1)
+
+    layer.middle(
+        xo, tdo, w, vec, att, xb, gw, sm, d_att, delta, dsa, hid, acc, ba,
+        tokens_ready, outputs_ready, lambda n: begin_after(scatter2, n), back_done,
+    )
 
     def small_send(i, src, device):
         t.send(
@@ -1215,27 +1263,28 @@
         )
 
     small_send(0, lambda: sm, at.sibling)
-
-    def back_steps(r):
-        @pl.when(r == 0)
+    scatter2.merge(2)
+    scatter2.merge(3)
+
+    def back_steps(n):
+        begin_after(scatter1, n)
+
+        @pl.when(n == 0)
         def _():
-            scatter2.step1(0)
-            scatter2.step1(1)
             t.landed(smb.at[0], sr.at[0])
             smb[3] = sm[...] + smb[0]
             small_send(1, lambda: smb.at[3], at.second_dev)
 
-        @pl.when(r == 1)
+        @pl.when(n == 1)
         def _():
-            scatter2.step1(2)
-            scatter2.step1(3)
             t.landed(smb.at[1], sr.at[1])
             smb[4] = smb[3] + smb[1]
             small_send(2, lambda: smb.at[4], at.first_dev)
-
-        @pl.when(r == 2)
+            scatter2.step2()
+            scatter1.merge(0)
+
+        @pl.when(n == 2)
         def _():
-            scatter2.step2(0)
             t.landed(smb.at[2], sr.at[2])
             smb[5] = smb[4] + smb[2]
             for k in range(1, ncol):
@@ -1245,16 +1294,15 @@
                     lambda to=to: smb.at[5, to], lambda k=k: smz.at[k],
                     lambda k=k: zs.at[k], lambda k=k: zr.at[k], at.col_dev(to),
                 )
-
-        @pl.when(r == 3)
+            scatter1.merge(1)
+
+        @pl.when(n == 3)
         def _():
-            scatter2.step2(1)
+            scatter1.merge(2)
 
     layer.attend_back(
         kv, kvt, qt, lse, delta, d_att, kvt, qt, p_scr, ds_scr, back_steps, (xp, xc, xo, gw)
     )
-    for i in range(4):
-        scatter1.begin(i)
 
     def grad_block(s):
         rows = rows_of(s)
@@ -1275,21 +1323,7 @@
     def grad_send(i):
         s = line.far[i]
         grad_block(s)
-
-        @pl.when(line.mid)
-        def _():
-            t.landed(gxz.at[s], gr.at[s])
-            gpb[i] = (dx[:, :PROMPT] + gxz[s].astype(F32)).astype(BF16)
-
-        @pl.when(line.end)
-        def _():
-            gpb[i] = dx[:, :PROMPT].astype(BF16)
-
-        t.send(
-            ("gx", i),
-            lambda: gpb.at[i], lambda: gxz.at[line.slot[i]],
-            lambda: gs.at[i], lambda: gr.at[line.slot[i]], at.col_dev(line.sum_to[i]),
-        )
+        x_sum.send(i, lambda: dx[:, :PROMPT])
         gcb[i] = dx[:, PROMPT:].astype(BF16)
         t.send(
             ("gc", i),
@@ -1298,74 +1332,94 @@
         )
 
     grad_send(0)
-    scatter2.step2(2)
-    for i in range(4):
-        scatter1.step1(i)
+    scatter1.merge(3)
+    scatter2.step3()
     grad_send(1)
-    scatter2.step2(3)
-    for i in range(4):
-        scatter1.step2(i)
+    scatter1.step2()
+    scatter1.step3()
     grad_send(2)
-    scatter2.step3(0)
-    scatter2.step3(1)
     grad_block(c)
-    gx_ref[:, :PROMPT] = dx[:, :PROMPT]
-    gx_ref[:, cont_cols(c, PROMPT)] = dx[:, PROMPT:]
-    scatter1.step3(0)
-    scatter1.step3(1)
-    scatter2.step3(2)
-    scatter1.step3(2)
+    gx_ref[...] = dx[:, :PROMPT]
+    gcb[3] = dx[:, PROMPT:].astype(BF16)
+    own_copies = [
+        pltpu.make_async_copy(xb.at[:, mine], xbo.at[:, :, own_cols(c)], bs.at[0]),
+        pltpu.make_async_copy(gcb.at[3], gco.at[c], kr.at[4]),
+    ]
+    own_copies[1].start()
 
     for k in range(1, ncol):
         t.landed(xbo.at[:, :, own_cols(at.behind(k))], br.at[k])
+    scatter2.step4()
+    scatter1.step4()
+    small = smb[5, c]
+    for k in range(1, ncol):
+        t.landed(smz.at[k], zr.at[k])
+        small = small + smz[k]
+    gv_ref[...] = small
+    for k in range(1, ncol):
+        s = at.behind(k)
+        t.landed(gco.at[s], kr.at[s])
+
+    def add_grad(value):
+        gx_ref[...] += value
+
+    x_sum.receive(add_grad)
+    scatter2.finish()
+    scatter1.finish()
+    for copy in own_copies:
+        copy.wait()
+    t.drain()
+
+
+def order_pieces(parts):
+    own, cont = GROUP // parts, NCONT * CONT // parts
+    pieces = []
+    for p in range(parts):
+        pieces.append((p * own, p * BLOCK, BLOCK))
+        pieces.append((p * own + BLOCK, (2 * parts - 1 - p) * BLOCK, BLOCK))
+        pieces.append((p * own + PAIR, PROMPT + p * cont, cont))
+    return pieces
+
+
+def finish_kernel(
+    parts, full, lens_ref, len_table, y_ref, ty_ref, xbo, gco, gp_ref, out1, out2, sums,
+    xout_ref, yout_ref, gx_ref, gy_ref, gq_ref, go_ref, gu_ref, gd_ref,
+    ga_ref, gb_ref, gc_ref, gd2_ref, loss_ref,
+):
+    group = lax.axis_index("dp") * lax.axis_size("row") + lax.axis_index("row")
+    count = jnp.sum(len_table[...].astype(F32))
     slot = iota((1, CONT), 1)
-    weight = jnp.concatenate(
-        [(iota((1, PROMPT), 1) < lens[0]).astype(F32)]
-        + [(slot < lens_ref[group, 1 + n]).astype(F32) for n in range(NCONT)],
-        axis=1,
-    ) * (total_tokens / count)
-    for frm, to, width in pieces:
+    live = [(iota((1, PROMPT), 1) < lens_ref[group, 0]).astype(F32)]
+    live += [(slot < lens_ref[group, 1 + n]).astype(F32) for n in range(NCONT)]
+    weight = jnp.concatenate(live, axis=1) * (lens_ref.shape[0] * GROUP / count)
+    for frm, to, width in order_pieces(parts):
         cols = slice(to, to + width)
         xout_ref[:, cols] = xbo[0, :, frm : frm + width]
         branch = xbo[1, :, frm : frm + width].astype(F32)
         y_here = y_ref[:, cols].astype(F32)
         yout_ref[:, cols] = (y_here + branch).astype(BF16)
         gy_ref[:, cols] = (y_here - ty_ref[:, cols].astype(F32) + branch) * weight[:, cols]
-
-    scatter2.step3(3)
-    scatter1.step3(3)
-    small = smb[5, c]
-    for k in range(1, ncol):
-        t.landed(smz.at[k], zr.at[k])
-        small = small + smz[k]
-    gv_ref[...] = small
-    for k in range(1, ncol):
-        s = at.behind(k)
-        t.landed(gco.at[s], kr.at[s])
-        gx_ref[:, cont_cols(s, PROMPT)] = gco[s].astype(F32)
-    for slot_at, cond in ((c, c > 0), (4, c < 3)):
-
-        @pl.when(cond)
-        def _(slot_at=slot_at):
-            t.landed(gxz.at[slot_at], gr.at[slot_at])
-            gx_ref[:, :PROMPT] += gxz[slot_at].astype(F32)
-
-    scatter2.finish()
-    scatter1.finish()
+    gx_ref[:, :PROMPT] = gp_ref[...]
+    cont = gco.shape[2]
+    for p in range(parts):
+        gx_ref[:, PROMPT + p * cont : PROMPT + (p + 1) * cont] = gco[p].astype(F32)
+    ff = gu_ref.shape[1]
     for i in range(3):
-        gq_ref[i] = out1[:, i * BLOCK : (i + 1) * BLOCK]
-    go_ref[...] = out2[:, :BLOCK].T
-    gu_ref[...] = out2[:, BLOCK : BLOCK + ff]
-    gd_ref[...] = out2[:, BLOCK + ff :].T
-    t.drain()
-
-
-def run_step(lengths, x, y, tx, ty, wq, wo, wu, wd, vec):
+        gq_ref[:, i, :] = out1[:, i * BLOCK : (i + 1) * BLOCK]
+    go_ref[...] = out1[:, 3 * BLOCK :].T
+    gu_ref[...] = out2[:, :ff]
+    gd_ref[...] = out2[:, ff:].T
+    for i, ref in enumerate((ga_ref, gb_ref, gc_ref, gd2_ref)):
+        ref[...] = sums[i : i + 1].reshape(ref.shape)
+    loss_ref[...] = sums[4:5, :1] / (2.0 * count * full)
+
+
+def run_step(lengths, x, y, tx, ty, wq, wo, wu, wd, vecs):
     feat, tokens = x.shape
     full = 4 * feat
     ff = wu.shape[1]
     width = 4 * BLOCK + 2 * ff
-    rest = BLOCK + 2 * ff
+    rest = 2 * ff
     half = feat // 2
     own, cont = tokens // 4, NCONT * CONT // 4
     keys = PROMPT + cont
@@ -1381,49 +1435,48 @@
 
     def reduce_buffers(cols):
         return [
-            bf(4, 4, half, cols), bf(2, 4, half, cols), bf(4, half, cols), bf(5, half, cols), f32(feat, cols),
+            bf(4, 4, half, cols), bf(2, 4, half, cols), bf(4, half, cols), bf(3, half, cols),
+            bf(3, half, cols),
         ]
 
     gather_sems = [
         dma((5,)), dma((4,)), dma((4,)), dma((4,)), dma((2, 4)), dma((2, 4)), dma((4, 4)), dma((4, 4)),
     ]
     scatter_sems = [
-        dma((4,)), dma((4,)), dma((2, 4)), dma((2, 4)), dma((4,)), dma((4,)), dma((3,)), dma((5,)),
+        dma((4,)), dma((4,)), dma((2,)), dma((2,)), dma(()), dma(()), dma((3,)), dma((3,)),
         dma(()), dma(()),
     ]
     sums = (4, 8, feat)
-    return pl.pallas_call(
+    smem, anywhere = pl.BlockSpec(memory_space=pltpu.SMEM), pl.BlockSpec(memory_space=pl.ANY)
+
+    def shape(*dims, dtype=F32):
+        return jax.ShapeDtypeStruct(dims, dtype)
+
+    raw = pl.pallas_call(
         functools.partial(step_kernel, 4),
         out_shape=(
-            jax.ShapeDtypeStruct((feat, tokens), BF16),
-            jax.ShapeDtypeStruct((feat, tokens), BF16),
-            jax.ShapeDtypeStruct((feat, tokens), F32),
-            jax.ShapeDtypeStruct((feat, tokens), F32),
-            jax.ShapeDtypeStruct((3, feat, BLOCK), F32),
-            jax.ShapeDtypeStruct(wo.shape, F32),
-            jax.ShapeDtypeStruct(wu.shape, F32),
-            jax.ShapeDtypeStruct(wd.shape, F32),
-            jax.ShapeDtypeStruct((8, feat), F32),
+            shape(2, feat, tokens, dtype=BF16), shape(4, feat, cont, dtype=BF16), shape(feat, PROMPT),
+            shape(feat, 4 * BLOCK), shape(feat, rest), shape(8, feat),
         ),
-        in_specs=[pl.BlockSpec(memory_space=pltpu.SMEM), vmem, pl.BlockSpec(memory_space=pl.ANY)]
-        + [vmem] * 8,
-        out_specs=[vmem] * 9,
+        in_specs=[smem, vmem] + [anywhere] * 4 + [vmem] * 8,
+        out_specs=[anywhere] * 2 + [vmem] * 4,
         scratch_shapes=[
-            bf(4, full, width), bf(4, full, width), bf(full, PROMPT), bf(full, cont), bf(full, own),
+            bf(feat, tokens), bf(feat, tokens), bf(feat, tokens),
+            bf(4, full, width), bf(4, 4, 2, half, width), bf(full, PROMPT), bf(full, cont), bf(full, own),
             bf(keys, full), bf(keys, 4 * PAIR), bf(4, PAIR, keys), bf(full, own), bf(full, own),
             f32(heads, own), f32(heads, own), bf(full, own), f32(2, PROMPT, PAIR), bf(2, PROMPT, PAIR),
             bf(2, PROMPT, own), bf(2, PROMPT, own), f32(full, own), bf(4, own, ff), f32(full, own),
             f32(full, own), f32(feat, keys), f32(feat, own), bf(2, feat, tokens), bf(2, full, own),
-            bf(2, full, own), bf(2, feat, tokens), f32(4, 8, feat), bf(3, feat, PROMPT),
-            bf(5, feat, PROMPT), bf(3, feat, cont), bf(4, feat, cont),
+            bf(2, full, own), f32(4, 8, feat), bf(3, feat, PROMPT),
+            bf(5, feat, PROMPT), bf(4, feat, cont),
             f32(*sums), f32(6, *sums), f32(*sums),
         ]
-        + reduce_buffers(3 * BLOCK)
+        + reduce_buffers(4 * BLOCK)
         + reduce_buffers(rest)
         + [
             dma((5,)), dma((4,)), dma((4,)), dma((4,)), dma((4,)), dma((4,)), dma((4,)), dma((4,)),
-            dma((4,)), dma((4,)), dma((3,)), dma((5,)), dma((3,)), dma((4,)), dma((3,)), dma((3,)),
-            dma((4,)), dma((4,)),
+            dma((4,)), dma((4,)), dma((3,)), dma((5,)), dma((3,)), dma((5,)), dma((3,)), dma((3,)),
+            dma((4,)), dma((4,)), dma((3,)),
         ]
         + gather_sems * 2
         + scatter_sems * 2,
@@ -1431,7 +1484,19 @@
             collective_id=2, has_side_effects=True, vmem_limit_bytes=61 << 20
         ),
         name="layer_step",
-    )(lengths, lengths, x, y, tx, ty, wq, wo, wu, wd, vec)
+    )(lengths, lengths, x, y, tx, ty, wq, wo, wu, wd, *vecs)
+    return pl.pallas_call(
+        functools.partial(finish_kernel, 4, full),
+        out_shape=(
+            shape(feat, tokens, dtype=BF16), shape(feat, tokens, dtype=BF16), shape(feat, tokens),
+            shape(feat, tokens), shape(*wq.shape), shape(*wo.shape), shape(*wu.shape),
+            shape(*wd.shape), shape(feat), shape(feat), shape(feat), shape(feat), shape(1, 1),
+        ),
+        in_specs=[smem] + [vmem] * 9,
+        out_specs=[vmem] * 13,
+        compiler_params=pltpu.CompilerParams(vmem_limit_bytes=61 << 20),
+        name="layer_results",
+    )(lengths, lengths, y, ty, *raw)
 
 
 def body(
@@ -1448,15 +1513,15 @@
     ff_block = w_up.shape[1]
 
     if ncol == parts:
-        small_vecs = jnp.stack([gain_attn, bias_attn, gain_ffn, bias_ffn] * 2).astype(F32)
-        x_out, y_out, grad_x, grad_y, g_q, g_o, g_u, g_d, sums = run_step(
-            lengths, x_stream, y_stream, teach_x, teach_y, w_qkv.reshape(feat, 3 * block),
-            w_out, w_up, w_down, small_vecs,
-        )
-        loss = sums[4, 0] / (2.0 * jnp.sum(lengths).astype(F32) * full)
+        (
+            x_out, y_out, grad_x, grad_y, g_q, g_o, g_u, g_d, g_ga, g_ba, g_gf, g_bf, loss,
+        ) = run_step(
+            lengths, x_stream, y_stream, teach_x, teach_y, w_qkv, w_out, w_up, w_down,
+            (gain_attn, bias_attn, gain_ffn, bias_ffn),
+        )
         return (
-            x_out, y_out, grad_x, grad_y, g_q.transpose(1, 0, 2), g_o, sums[0], sums[1], g_u, g_d,
-            sums[2], sums[3], loss,
+            x_out, y_out, grad_x, grad_y, g_q, g_o, g_ga, g_ba, g_u, g_d, g_gf, g_bf,
+            loss.reshape(()),
         )
 
     y_f32 = y_stream.astype(F32)

time: 169 us -> 151 us (0.89); the launches traced: 167 us -> 151 us
  local copies, waits for them, and re-layouts: 13.6 us -> 3.27 us
  between operations: 3.16 us -> 0.66 us
  other arithmetic: 1.92 us -> 0 us
    unnamed x33 -> x2, local copies, waits for them, and re-layouts: 11.1 us -> 3.27 us
    pallas_call x1 -> x2, Pallas kernels: 148 us -> 147 us  [the longest x1 143 us: run_step(): pl.pallas_call(functools.partial(step_kernel, 4), out_shape=(shape(2, fea...]
where the time goes in v2:
time: 151 us
  Pallas kernels  147 us (97%)
  local copies, waits for them, and re-layouts  3.27 us (2%)
    pallas_call x1, Pallas kernels, run_step(): pl.pallas_call(functools.partial(step_kernel, 4), out_shape=(shape(2, fea...  143 us
    pallas_call x1, Pallas kernels, run_step(): pl.pallas_call(functools.partial(finish_kernel, 4, full), out_shape=(shap...  4.43 us
    unnamed x2, local copies, waits for them, and re-layouts  3.27 us

profile of v2, /device:TPU:13, one launch (start us, length us, event | category | flops | bytes accessed | tf_op | source)
XLA Modules:
  0.0 151.2 jit_solution(12546957578582561778)
XLA Ops:
  0.6 1.6 %copy.26.wq_ref = bf16[128,3,128]{2,1,0:T(4,128)(2,1)} copy(bf16[128,3,128]{2,0,1:T(8,128)(2,1)} %param.15) | data formatting | bytes 196608 | tf_op args[2]
  2.3 142.8 %layer_step.1 = (bf16[2,128,2048]{2,1,0:T(8,128)(2,1)}, bf16[4,128,256]{2,1,0:T(8,128)(2,1)}, f32[128,1024]{1,0:T(8,128)}, f32[128,512]{1,0:T(8,128)}, f32[128,1024]{1,0:T(8,128)}, /*index=5*/f32[8,128]{1,0:T(8,128)}) custom-call(s32[8,9]{1,0:T(8,128)} %len_table.3, s32[8,9]{1,0:T(8,128)} %len_table.3, bf16[128,2048]{1,0:T(8,128)(2,1)} %x_ref.1, ...), custom_call_target="tpu_custom_call" | custom-call | tf_op jit(solution)/shard_map/layer_step/pallas_call | solution.py:1455
  145.1 4.4 %layer_results.1 = (bf16[128,2048]{1,0:T(8,128)(2,1)}, bf16[128,2048]{1,0:T(8,128)(2,1)}, f32[128,2048]{1,0:T(8,128)}, f32[128,2048]{1,0:T(8,128)}, f32[128,3,12...) custom-call(s32[8,9]{1,0:T(8,128)} %len_table.3, ...), custom_call_target="tpu_custom_call" | custom-call | tf_op jit(solution)/shard_map/layer_results/pallas_call | solution.py:1488
  149.6 1.6 %copy.27 = f32[128,3,128]{2,0,1:T(8,128)} copy(f32[128,3,128]{2,1,0:T(4,128)} %get-tuple-element.55) | data formatting | bytes 393216

commit v3 on v2

--- a/solution.py
+++ b/solution.py
@@ -615,7 +615,8 @@
         lax.fori_loop(0, kvt.shape[0], step, 0)
 
     def attend_back(
-        self, kv, kvt, qt, lse, delta, d_att, dkvt, dqt, p_scr, ds_scr, between=None, grads=None
+        self, kv, kvt, qt, lse, delta, d_att, dkvt, dqt, p_scr, ds_scr, between=None, grads=None,
+        inputs=None,
     ):
         def step(n, carry):
             r = self.order(n)
@@ -660,6 +661,10 @@
                 dkvt[r, v_rows, :PROMPT] = dot_nt(d_mine, p_scr[head]).astype(BF16)
             if grads is not None:
                 self.projection_grads(r, pair, *grads, dkvt, dqt)
+            if inputs is not None:
+                w, dx, dxo = inputs
+                dx[...] += dot_nn(w[r, :, BLOCK : 3 * BLOCK], dkvt[r])
+                dxo[...] += dot_nn(w[r, :, :BLOCK], dqt[pair])
             if between is not None:
                 between(n)
             return carry
@@ -959,25 +964,28 @@
         self.out, self.landing = out, landing
         self.send_s, self.recv_s = sems
 
-    def send(self, i, value):
+    def move(self, i, cond):
         line = self.line
-        s = line.far[i]
-
-        @pl.when(line.mid)
+        self.t.send(
+            (self.tag, "col", i, cond is line.mid),
+            lambda: self.out.at[i], lambda: self.landing.at[line.slot[i]],
+            lambda: self.send_s.at[i], lambda: self.recv_s.at[line.slot[i]],
+            self.t.at.col_dev(line.sum_to[i]), cond,
+        )
+
+    def put(self, i, value):
+        self.out[i] = value.astype(BF16)
+        self.move(i, self.line.end)
+
+    def relay(self, i):
+        s = self.line.far[i]
+
+        @pl.when(self.line.mid)
         def _():
             self.t.landed(self.landing.at[s], self.recv_s.at[s])
-            self.out[i] = (value() + self.landing[s].astype(F32)).astype(BF16)
-
-        @pl.when(line.end)
-        def _():
-            self.out[i] = value().astype(BF16)
-
-        self.t.send(
-            (self.tag, "col", i),
-            lambda: self.out.at[i], lambda: self.landing.at[line.slot[i]],
-            lambda: self.send_s.at[i], lambda: self.recv_s.at[line.slot[i]],
-            self.t.at.col_dev(line.sum_to[i]),
-        )
+            self.out[i] = self.out[i] + self.landing[s]
+
+        self.move(i, self.line.mid)
 
     def receive(self, add):
         for slot, cond in ((self.line.c, self.line.c > 0), (4, self.line.c < 3)):
@@ -1041,21 +1049,22 @@
     def step3(self):
         self.t.landed(self.two.at[0], self.two_r.at[0])
         self.t.landed(self.one, self.one_r)
-        for k in range(1, 4):
-            to = self.at.ahead(k)
-            self.zs[k - 1] = self.total(to).astype(BF16)
+        c = self.line.c
+        for i in range(3):
+            to = self.line.far[i]
+            self.zs[i] = self.total(to).astype(BF16)
             self.t.send(
-                (self.tag, "col", k),
-                lambda k=k: self.zs.at[k - 1], lambda k=k: self.zb.at[k - 1],
-                lambda k=k: self.col_s.at[k - 1], lambda k=k: self.col_r.at[k - 1], self.at.col_dev(to),
+                (self.tag, "col", i),
+                lambda i=i: self.zs.at[i], lambda: self.zb.at[c],
+                lambda i=i: self.col_s.at[i], lambda: self.col_r.at[c], self.at.col_dev(to),
             )
 
     def step4(self):
         mine = pl.ds(pl.multiple_of(self.at.dp * self.half, self.half), self.half)
         total = self.total(self.line.c)
-        for k in range(3):
-            self.t.landed(self.zb.at[k], self.col_r.at[k])
-            total = total + self.zb[k].astype(F32)
+        for s in self.line.near[1:]:
+            self.t.landed(self.zb.at[s], self.col_r.at[s])
+            total = total + self.zb[s].astype(F32)
         self.out[mine] = total
         self.t.send(
             (self.tag, "fin"),
@@ -1073,7 +1082,7 @@
     va_ref, vb_ref, vc_ref, vd_ref,
     xbo, gco, gx_ref, out1, out2, gv_ref,
     y_ref, tx_ref, ty_ref, w, gw, xp, xc, xo, xt, kv, kvt, qt, att, lse, delta, d_att, s_scr, pf_scr, p_scr, ds_scr,
-    dsa, hid, acc, ba, dx, dxo, tdp, tdo, xb, vrow, gpb, gxz, gcb, sm, smb, smz,
+    dsa, hid, acc, ba, dx, tdp, tdo, xb, vrow, gpb, gxz, gcb, sm, smb, smz,
     sib1, two1, one1, zs1, zb1, sib2, two2, one2, zs2, zb2,
     xs, xr, cs, cr, ts, tr, vs, vr, bs, br, gs, gr, ks, kr, ss, sr, zs, zr, ls, *wsems,
 ):
@@ -1122,16 +1131,9 @@
             lambda i=i: xs.at[i], lambda: xr.at[c],
             at.col_dev(line.near[1 + i]), line.mid if i else None,
         )
-    for k in range(1, ncol):
-        to = at.ahead(k)
-        t.send(
-            ("xc", k),
-            lambda to=to: x_ref.at[:, cont_cols(to, PROMPT)], lambda: xc.at[mine],
-            lambda k=k: cs.at[k], lambda k=k: cr.at[k], at.col_dev(to),
-        )
     local = [
-        lambda: pltpu.make_async_copy(x_ref.at[:, :PROMPT], xp.at[mine], cs.at[0]),
-        lambda: pltpu.make_async_copy(x_ref.at[:, cont_cols(c, PROMPT)], xc.at[mine], cr.at[0]),
+        lambda: pltpu.make_async_copy(x_ref.at[:, :PROMPT], xp.at[mine], ls.at[3]),
+        lambda: pltpu.make_async_copy(x_ref.at[:, cont_cols(c, PROMPT)], xc.at[mine], ls.at[4]),
     ]
     for make in local:
         make().start()
@@ -1164,25 +1166,32 @@
 
     gather1.arrive(1)
     gather1.arrive(2)
+    gather1.first(0)
     gather2.arrive(1)
     gather2.arrive(2)
-    gather1.first(0)
     gather2.first(0)
     gather1.arrive(3)
+    gather1.first(1)
+    gather1.first(2)
     gather2.arrive(3)
     x_arrive(1)
     x_arrive(2)
-    for j in range(1, 4):
-        gather1.first(j)
-    for j in range(4):
-        gather1.second(j)
+    for k, to in enumerate(line.near[1:]):
+        t.send(
+            ("xc", k),
+            lambda to=to: x_ref.at[:, cont_cols(to, PROMPT)], lambda: xc.at[mine],
+            lambda k=k: cs.at[k], lambda: cr.at[c], at.col_dev(to),
+        )
     gather2.first(1)
+    gather1.first(3)
     gather2.first(2)
-    gather2.second(0)
+    gather1.second(0)
+    gather1.second(1)
+    gather1.second(2)
+    gather1.second(3)
     x_arrive(3)
-    gather2.first(3)
-    for k in range(1, ncol):
-        t.landed(xc.at[rows_of(at.behind(k))], cr.at[k])
+    for s in line.near[1:]:
+        t.landed(xc.at[rows_of(s)], cr.at[s])
     for make in local:
         make().wait()
     gather1.finish()
@@ -1194,25 +1203,29 @@
     layer = Layer(c, parts, lens, total_tokens, count, functools.partial(row_order, at.row))
     layer.project(xp, xc, w, xo, xt, kv, kvt, qt)
 
-    for k in range(1, ncol):
-        to = at.ahead(k)
+    for k, to in enumerate(line.near[1:]):
         t.send(
             ("td", k),
             lambda to=to: tdp.at[:, :, own_cols(to)], lambda: tdo.at[:, mine],
-            lambda k=k: ts.at[k], lambda k=k: tr.at[k], at.col_dev(to),
+            lambda k=k: ts.at[k], lambda: tr.at[c], at.col_dev(to),
         )
     tdo[:, mine] = tdp[:, :, own_cols(c)]
 
     def forward_steps(r):
         @pl.when(r == 0)
         def _():
-            gather2.second(1)
+            gather2.first(3)
 
         @pl.when(r == 1)
         def _():
+            gather2.second(0)
+            gather2.second(1)
+
+        @pl.when(r == 2)
+        def _():
             gather2.second(2)
 
-        @pl.when(r == 2)
+        @pl.when(r == 3)
         def _():
             gather2.second(3)
 
@@ -1223,18 +1236,17 @@
     vec = jnp.concatenate([vrow[s].T for s in range(ncol)], axis=0)
 
     def tokens_ready():
-        for k in range(1, ncol):
-            t.landed(tdo.at[:, rows_of(at.behind(k))], tr.at[k])
+        for s in line.near[1:]:
+            t.landed(tdo.at[:, rows_of(s)], tr.at[s])
 
     def outputs_ready():
-        for k in range(1, ncol):
-            to = at.ahead(k)
+        for k, to in enumerate(line.near[1:]):
             t.send(
                 ("xb", k),
                 lambda to=to: xb.at[:, rows_of(to)], lambda: xbo.at[:, :, own_cols(c)],
-                lambda k=k: bs.at[k], lambda k=k: br.at[k], at.col_dev(to),
-            )
-        pltpu.make_async_copy(xb.at[:, mine], xbo.at[:, :, own_cols(c)], bs.at[0]).start()
+                lambda k=k: bs.at[k], lambda: br.at[c], at.col_dev(to),
+            )
+        pltpu.make_async_copy(xb.at[:, mine], xbo.at[:, :, own_cols(c)], ls.at[5]).start()
 
     scatter1 = WeightScatter(
         "g1", t, line, gw, near, sib1, two1, one1, zs1, zb1, out1, wsems[16:26]
@@ -1299,32 +1311,24 @@
         @pl.when(n == 3)
         def _():
             scatter1.merge(2)
-
+            scatter1.step2()
+
+    dx[...] = jnp.zeros_like(dx)
+    acc[...] = dsa[...]
     layer.attend_back(
-        kv, kvt, qt, lse, delta, d_att, kvt, qt, p_scr, ds_scr, back_steps, (xp, xc, xo, gw)
+        kv, kvt, qt, lse, delta, d_att, kvt, qt, p_scr, ds_scr, back_steps, (xp, xc, xo, gw),
+        (w, dx, acc),
     )
 
-    def grad_block(s):
-        rows = rows_of(s)
-        for r in range(w.shape[0]):
-            part = dot_nn(w[r, rows, BLOCK : 3 * BLOCK], kvt[r])
-            mine_part = dot_nn(w[r, rows, :BLOCK], qt[r * BLOCK : (r + 1) * BLOCK])
-            if r == 0:
-                dx[...] = part
-                dxo[...] = dsa[rows] + mine_part
-            else:
-                dx[...] += part
-                dxo[...] += mine_part
-        low, high = layer.own_columns()
-        dx[:, low] += dxo[:, :BLOCK]
-        dx[:, high] += dxo[:, BLOCK:PAIR]
-        dx[:, PROMPT:] += dxo[:, PAIR:]
+    low, high = layer.own_columns()
+    dx[:, low] += acc[:, :BLOCK]
+    dx[:, high] += acc[:, BLOCK:PAIR]
+    dx[:, PROMPT:] += acc[:, PAIR:]
 
     def grad_send(i):
         s = line.far[i]
-        grad_block(s)
-        x_sum.send(i, lambda: dx[:, :PROMPT])
-        gcb[i] = dx[:, PROMPT:].astype(BF16)
+        x_sum.put(i, dx[rows_of(s), :PROMPT])
+        gcb[i] = dx[rows_of(s), PROMPT:].astype(BF16)
         t.send(
             ("gc", i),
             lambda: gcb.at[i], lambda: gco.at[c],
@@ -1335,20 +1339,21 @@
     scatter1.merge(3)
     scatter2.step3()
     grad_send(1)
-    scatter1.step2()
-    scatter1.step3()
     grad_send(2)
-    grad_block(c)
-    gx_ref[...] = dx[:, :PROMPT]
-    gcb[3] = dx[:, PROMPT:].astype(BF16)
+    gx_ref[...] = dx[mine, :PROMPT]
+    gcb[3] = dx[mine, PROMPT:].astype(BF16)
     own_copies = [
-        pltpu.make_async_copy(xb.at[:, mine], xbo.at[:, :, own_cols(c)], bs.at[0]),
-        pltpu.make_async_copy(gcb.at[3], gco.at[c], kr.at[4]),
+        pltpu.make_async_copy(xb.at[:, mine], xbo.at[:, :, own_cols(c)], ls.at[5]),
+        pltpu.make_async_copy(gcb.at[3], gco.at[c], ls.at[6]),
     ]
     own_copies[1].start()
-
-    for k in range(1, ncol):
-        t.landed(xbo.at[:, :, own_cols(at.behind(k))], br.at[k])
+    x_sum.relay(0)
+    scatter1.step3()
+    x_sum.relay(1)
+    x_sum.relay(2)
+
+    for s in line.near[1:]:
+        t.landed(xbo.at[:, :, own_cols(s)], br.at[s])
     scatter2.step4()
     scatter1.step4()
     small = smb[5, c]
@@ -1436,14 +1441,14 @@
     def reduce_buffers(cols):
         return [
             bf(4, 4, half, cols), bf(2, 4, half, cols), bf(4, half, cols), bf(3, half, cols),
-            bf(3, half, cols),
+            bf(4, half, cols),
         ]
 
     gather_sems = [
         dma((5,)), dma((4,)), dma((4,)), dma((4,)), dma((2, 4)), dma((2, 4)), dma((4, 4)), dma((4, 4)),
     ]
     scatter_sems = [
-        dma((4,)), dma((4,)), dma((2,)), dma((2,)), dma(()), dma(()), dma((3,)), dma((3,)),
+        dma((4,)), dma((4,)), dma((2,)), dma((2,)), dma(()), dma(()), dma((3,)), dma((4,)),
         dma(()), dma(()),
     ]
     sums = (4, 8, feat)
@@ -1466,7 +1471,7 @@
             bf(keys, full), bf(keys, 4 * PAIR), bf(4, PAIR, keys), bf(full, own), bf(full, own),
             f32(heads, own), f32(heads, own), bf(full, own), f32(2, PROMPT, PAIR), bf(2, PROMPT, PAIR),
             bf(2, PROMPT, own), bf(2, PROMPT, own), f32(full, own), bf(4, own, ff), f32(full, own),
-            f32(full, own), f32(feat, keys), f32(feat, own), bf(2, feat, tokens), bf(2, full, own),
+            f32(full, own), f32(full, keys), bf(2, feat, tokens), bf(2, full, own),
             bf(2, full, own), f32(4, 8, feat), bf(3, feat, PROMPT),
             bf(5, feat, PROMPT), bf(4, feat, cont),
             f32(*sums), f32(6, *sums), f32(*sums),
@@ -1476,7 +1481,7 @@
         + [
             dma((5,)), dma((4,)), dma((4,)), dma((4,)), dma((4,)), dma((4,)), dma((4,)), dma((4,)),
             dma((4,)), dma((4,)), dma((3,)), dma((5,)), dma((3,)), dma((5,)), dma((3,)), dma((3,)),
-            dma((4,)), dma((4,)), dma((3,)),
+            dma((4,)), dma((4,)), dma((7,)),
         ]
         + gather_sems * 2
         + scatter_sems * 2,

time: 151 us -> 142 us (0.940); the launches traced: 151 us -> 140 us
  Pallas kernels: 147 us -> 136 us
    pallas_call x1, Pallas kernels: 143 us -> 132 us  [run_step(): pl.pallas_call(functools.partial(step_kernel, 4), out_shape=(shape(2, fea...]
where the time goes in v3:
time: 142 us; the launch traced here: 140 us
  Pallas kernels  136 us (96%)
  local copies, waits for them, and re-layouts  3.27 us (2%)
    pallas_call x1, Pallas kernels, run_step(): pl.pallas_call(functools.partial(step_kernel, 4), out_shape=(shape(2, fea...  132 us
    pallas_call x1, Pallas kernels, run_step(): pl.pallas_call(functools.partial(finish_kernel, 4, full), out_shape=(shap...  4.43 us
    unnamed x2, local copies, waits for them, and re-layouts  3.27 us

profile of v3, /device:TPU:13, one launch (start us, length us, event | category | flops | bytes accessed | tf_op | source)
XLA Modules:
  0.0 140.4 jit_solution(16500914883503481968)
XLA Ops:
  0.6 1.6 %copy.26.wq_ref = bf16[128,3,128]{2,1,0:T(4,128)(2,1)} copy(bf16[128,3,128]{2,0,1:T(8,128)(2,1)} %param.15) | data formatting | bytes 196608 | tf_op args[2]
  2.3 132.0 %layer_step.1 = (bf16[2,128,2048]{2,1,0:T(8,128)(2,1)}, bf16[4,128,256]{2,1,0:T(8,128)(2,1)}, f32[128,1024]{1,0:T(8,128)}, f32[128,512]{1,0:T(8,128)}, f32[128,1024]{1,0:T(8,128)}, /*index=5*/f32[8,128]{1,0:T(8,128)}) custom-call(s32[8,9]{1,0:T(8,128)} %len_table.3, s32[8,9]{1,0:T(8,128)} %len_table.3, bf16[128,2048]{1,0:T(8,128)(2,1)} %x_ref.1, ...), custom_call_target="tpu_custom_call" | custom-call | tf_op jit(solution)/shard_map/layer_step/pallas_call | solution.py:1460
  134.3 4.4 %layer_results.1 = (bf16[128,2048]{1,0:T(8,128)(2,1)}, bf16[128,2048]{1,0:T(8,128)(2,1)}, f32[128,2048]{1,0:T(8,128)}, f32[128,2048]{1,0:T(8,128)}, f32[128,3,12...) custom-call(s32[8,9]{1,0:T(8,128)} %len_table.3, ...), custom_call_target="tpu_custom_call" | custom-call | tf_op jit(solution)/shard_map/layer_results/pallas_call | solution.py:1493
  138.7 1.6 %copy.27 = f32[128,3,128]{2,0,1:T(8,128)} copy(f32[128,3,128]{2,1,0:T(4,128)} %get-tuple-element.55) | data formatting | bytes 393216

commit v4 on v3

--- a/solution.py
+++ b/solution.py
@@ -1201,8 +1201,6 @@
     count = jnp.sum(len_table[...].astype(F32))
     total_tokens = lens_ref.shape[0] * GROUP
     layer = Layer(c, parts, lens, total_tokens, count, functools.partial(row_order, at.row))
-    layer.project(xp, xc, w, xo, xt, kv, kvt, qt)
-
     for k, to in enumerate(line.near[1:]):
         t.send(
             ("td", k),
@@ -1210,6 +1208,8 @@
             lambda k=k: ts.at[k], lambda: tr.at[c], at.col_dev(to),
         )
     tdo[:, mine] = tdp[:, :, own_cols(c)]
+    layer.project(xp, xc, w, xo, xt, kv, kvt, qt)
+
 
     def forward_steps(r):
         @pl.when(r == 0)

time: 142 us -> 140 us (0.986); the launches traced: 140 us -> 140 us
  no operation moved by 1% of the time
where the time goes in v4:
time: 140 us
  Pallas kernels  136 us (97%)
  local copies, waits for them, and re-layouts  3.27 us (2%)
    pallas_call x1, Pallas kernels, run_step(): pl.pallas_call(functools.partial(step_kernel, 4), out_shape=(shape(2, fea...  132 us
    pallas_call x1, Pallas kernels, run_step(): pl.pallas_call(functools.partial(finish_kernel, 4, full), out_shape=(shap...  4.43 us
    unnamed x2, local copies, waits for them, and re-layouts  3.27 us

profile of v4, /device:TPU:13, one launch (start us, length us, event | category | flops | bytes accessed | tf_op | source)
XLA Modules:
  0.0 140.2 jit_solution(8833481375521968381)
XLA Ops:
  0.6 1.6 %copy.26.wq_ref = bf16[128,3,128]{2,1,0:T(4,128)(2,1)} copy(bf16[128,3,128]{2,0,1:T(8,128)(2,1)} %param.15) | data formatting | bytes 196608 | tf_op args[2]
  2.3 131.9 %layer_step.1 = (bf16[2,128,2048]{2,1,0:T(8,128)(2,1)}, bf16[4,128,256]{2,1,0:T(8,128)(2,1)}, f32[128,1024]{1,0:T(8,128)}, f32[128,512]{1,0:T(8,128)}, f32[128,1024]{1,0:T(8,128)}, /*index=5*/f32[8,128]{1,0:T(8,128)}) custom-call(s32[8,9]{1,0:T(8,128)} %len_table.3, s32[8,9]{1,0:T(8,128)} %len_table.3, bf16[128,2048]{1,0:T(8,128)(2,1)} %x_ref.1, ...), custom_call_target="tpu_custom_call" | custom-call | tf_op jit(solution)/shard_map/layer_step/pallas_call | solution.py:1460
  134.2 4.4 %layer_results.1 = (bf16[128,2048]{1,0:T(8,128)(2,1)}, bf16[128,2048]{1,0:T(8,128)(2,1)}, f32[128,2048]{1,0:T(8,128)}, f32[128,2048]{1,0:T(8,128)}, f32[128,3,12...) custom-call(s32[8,9]{1,0:T(8,128)} %len_table.3, ...), custom_call_target="tpu_custom_call" | custom-call | tf_op jit(solution)/shard_map/layer_results/pallas_call | solution.py:1493
  138.6 1.6 %copy.27 = f32[128,3,128]{2,0,1:T(8,128)} copy(f32[128,3,128]{2,1,0:T(4,128)} %get-tuple-element.55) | data formatting | bytes 393216
